TPU v7x, 256 devices: a whole 4x4x8 slice. The times are simulated.
256 devices in a mesh: grid: 32 (over z, x_hi, core), orb: 8 (over y, x_lo).
Axes of the slice: x: 4 (x_hi: 2, x_lo: 2; x = x_hi * 2 + x_lo), y: 4, z: 8, core: 2. Of those that a mesh axis runs over, the one named last changes fastest.
Arguments:
- wave: float32 [2, 8, 128, 128, 128], P(None, 'orb', 'grid'), may hold values from -6 to 6
- potential: float32 [128, 128, 128], P('grid'), may hold values from -24 to 24
- occupations: float32 [8], P('orb'), may hold values from 0.01 to 0.1
- centres: int32 [3, 128], replicated, may hold values from 0 to 127, as said below
- species: int32 [128], replicated, may hold values from 0 to 1
- projectors: float32 [2, 16, 8, 256], replicated, may hold values from -0.75 to 0.75
- coupling: float32 [2, 8, 8], replicated, may hold values from -6 to 6
Outputs:
- update: float32 [2, 8, 128, 128, 128], P(None, 'orb', 'grid')
- density: float32 [128, 128, 128], P('grid', 'orb')
Inputs may be any that keep to these rules, and one draw needn't show every extreme that they name: `centres`: each column is a grid point of the cell.
All inputs are finite; a program needn't handle non-finite values.
Results may differ from a plain program's by a relative error of at most 0.0003.
Values sent between devices are 32-bit elements; how exact they have to be, the bound alone decides.
No kernel may reach another device: no remote copies, remote signals or barrier semaphores. Data moves between devices by JAX's collectives and lax.ppermute only.
A program may use at most 64 MiB of HBM per device.

v0:
```python
import math

import jax
import jax.numpy as jnp
import numpy as np
from jax import lax
from jax.experimental import pallas as pl
from jax.experimental.pallas import tpu as pltpu
from jax.sharding import PartitionSpec as P


spacing = 0.32
time_step = 0.1
highest = lax.Precision.HIGHEST

SIDE = 128
BOX = 16
NPROJ = 8
PLANES = 4
PAD = SIDE + BOX
GROUP = 4
F32 = jnp.float32
BF16 = jnp.bfloat16


def permuted(value, axis, target):
    count = lax.axis_size(axis)
    return lax.ppermute(value, axis, [(source, target(source) % count) for source in range(count)])


def kinetic_matrix(extent):
    counts = np.arange(extent)
    signed = np.where(counts < extent // 2, counts, counts - extent)
    waves = signed * (2.0 * math.pi / (extent * spacing))
    angles = (counts[:, None] * counts[None, :] % extent) * (2.0 * math.pi / extent)
    column = (np.cos(angles) * (0.5 * waves**2)[None, :]).sum(axis=1) / extent
    return column[(counts[:, None] - counts[None, :]) % extent]


def kinetic_halves(extent):
    matrix = kinetic_matrix(extent).astype(np.float32)
    high = matrix.astype(BF16)
    low = (matrix - high.astype(np.float32)).astype(BF16)
    row = np.concatenate([high, low], axis=1)
    return jnp.asarray(np.concatenate([row, row], axis=0))


def halves(value):
    high = value.astype(BF16)
    return high, (value - high.astype(F32)).astype(BF16)


def times_right(value, wide):
    product = jnp.dot(jnp.concatenate(halves(value), axis=1), wide, preferred_element_type=F32)
    return product[:, :SIDE] + product[:, SIDE:]


def times_left(pair, value):
    row = jnp.concatenate(halves(value), axis=1)
    product = jnp.dot(pair, jnp.concatenate([row, row], axis=0), preferred_element_type=F32)
    return product[:, :SIDE] + product[:, SIDE:]


def whole(memory=pltpu.VMEM):
    return pl.BlockSpec(memory_space=memory)


def call(kernel, out_shape, specs, scratch=(), outs=None, flops=1000000, moved=1000000):
    return pl.pallas_call(
        kernel,
        out_shape=out_shape,
        in_specs=specs,
        out_specs=jax.tree.map(lambda _: whole(), out_shape) if outs is None else outs,
        scratch_shapes=list(scratch),
        compiler_params=pltpu.CompilerParams(vmem_limit_bytes=12 * 1024 * 1024),
        cost_estimate=pl.CostEstimate(flops=flops, bytes_accessed=moved, transcendentals=0),
    )


def shape(*dims):
    return jax.ShapeDtypeStruct(dims, F32)


def density_kernel(occupation_ref, wave_ref, out_ref):
    occupation = occupation_ref[0]
    for plane in range(PLANES):
        real_part = wave_ref[0, plane]
        imag_part = wave_ref[1, plane]
        term = occupation * (real_part * real_part + imag_part * imag_part)
        for share in range(8):
            high, middle, low = share // 4, share // 2 % 2, share % 2
            out_ref[middle, high, low, plane] = term[share * 16 : share * 16 + 16]


def swap_blocks(tile, lane, row):
    for bit in (1, 2, 4):
        row_set = (row & bit) != 0
        lane_set = ((lane >> 4) & bit) != 0
        up = pltpu.roll(pltpu.roll(tile, 8 - bit, 0), 16 * bit, 1)
        down = pltpu.roll(pltpu.roll(tile, bit, 0), SIDE - 16 * bit, 1)
        tile = jnp.where(row_set == lane_set, tile, jnp.where(lane_set, up, down))
    return tile


def atom_place(first_ref, centres_ref, atom):
    depth = (first_ref[0] - centres_ref[0, atom] + (BOX // 2 + SIDE)) & (SIDE - 1)
    start_y = (centres_ref[1, atom] + (SIDE - BOX // 2)) & (SIDE - 1)
    start_z = (centres_ref[2, atom] + (SIDE - BOX // 2)) & (SIDE - 1)
    touched = ((depth + (PLANES - 1)) & (SIDE - 1)) < BOX + PLANES - 1
    return depth, start_y, start_z, touched


def table_row(depth, plane, kind):
    slot = (depth + plane) & (SIDE - 1)
    return jnp.where(slot < BOX, kind * BOX + slot, 2 * BOX)


def project_kernel(
    first_ref, centres_ref, species_ref, wave_ref, projectors_ref, coef_ref, table_ref, listed_ref, padded, sums
):
    lane = lax.broadcasted_iota(jnp.int32, (8, SIDE), 1)
    row = lax.broadcasted_iota(jnp.int32, (8, SIDE), 0)
    for index in range(2 * PLANES):
        padded[index, 0:SIDE, :] = wave_ref[index]
        padded[index, SIDE:PAD, :] = wave_ref[index, 0:BOX, :]
    sums[...] = jnp.zeros_like(sums)

    def list_step(atom, count):
        touched = atom_place(first_ref, centres_ref, atom)[3]
        listed_ref[count] = atom
        return count + touched.astype(jnp.int32)

    count = lax.fori_loop(0, SIDE, list_step, 0, unroll=8)
    listed_ref[SIDE + GROUP] = count
    for extra in range(GROUP):
        listed_ref[count + extra] = SIDE

    for index in range(2 * BOX):
        for half in range(2):
            tile = projectors_ref[index, :, half * SIDE : (half + 1) * SIDE]
            table_ref[index, half * 8 : half * 8 + 8, :] = swap_blocks(tile, lane, row)
    table_ref[2 * BOX] = jnp.zeros((BOX, SIDE), F32)
    inner = lane & (BOX - 1)

    def group_step(step, carry):
        for offset in range(GROUP):
            listed = listed_ref[step * GROUP + offset]
            atom = jnp.minimum(listed, SIDE - 1)
            depth, start_y, start_z, _ = atom_place(first_ref, centres_ref, atom)
            kind = species_ref[atom]
            picks = (inner + start_z) & (SIDE - 1)
            totals = [jnp.zeros((8, SIDE), F32), jnp.zeros((8, SIDE), F32)]
            for plane in range(PLANES):
                index = table_row(depth, plane, kind)
                for half in range(2):
                    weights = table_ref[index, half * 8 : half * 8 + 8, :]
                    for part in range(2):
                        values = padded[part * PLANES + plane, pl.ds(start_y + half * 8, 8), :]
                        values = jnp.take_along_axis(values, picks, axis=1)
                        totals[part] = totals[part] + values * weights
            for part in range(2):
                sums[part, pl.ds(listed, 1), :] = jnp.sum(totals[part], axis=0, keepdims=True)
        return carry

    lax.fori_loop(0, (count + (GROUP - 1)) // GROUP, group_step, 0)
    group_row = lax.broadcasted_iota(jnp.int32, (NPROJ, SIDE), 0)
    group_lane = lax.broadcasted_iota(jnp.int32, (NPROJ, SIDE), 1)
    groups = (group_lane >> 4 == group_row).astype(F32)
    for part in range(2):
        coef_ref[part * 8 : part * 8 + 8, :] = lax.dot_general(
            groups,
            sums[part, 0:SIDE, :],
            (((1,), (1,)), ((), ())),
            precision=highest,
            preferred_element_type=F32,
        )


def spread_kernel(
    first_ref,
    centres_ref,
    species_ref,
    listed_ref,
    coef_ref,
    coupling_ref,
    table_ref,
    local_ref,
    out_ref,
    padded,
    scaled,
):
    lane = lax.broadcasted_iota(jnp.int32, (8, SIDE), 1)
    groups = (lane >> 4 == lax.broadcasted_iota(jnp.int32, (8, SIDE), 0)).astype(F32)
    for kind in range(2):
        mixing = lax.dot_general(
            coupling_ref[kind], groups, (((0,), (0,)), ((), ())), precision=highest, preferred_element_type=F32
        )
        for part in range(2):
            scaled[kind, part] = lax.dot_general(
                coef_ref[part * 8 : part * 8 + 8, :],
                mixing,
                (((0,), (0,)), ((), ())),
                precision=highest,
                preferred_element_type=F32,
            )
    for index in range(2 * PLANES):
        padded[index, 0:SIDE, :] = local_ref[index]
        padded[index, SIDE:PAD, :] = jnp.zeros((BOX, SIDE), F32)

    def group_step(step, carry):
        for offset in range(GROUP):
            listed = listed_ref[step * GROUP + offset]
            atom = jnp.minimum(listed, SIDE - 1)
            depth, start_y, start_z, _ = atom_place(first_ref, centres_ref, atom)
            kind = species_ref[atom]
            inside = ((lane - start_z) & (SIDE - 1)) < jnp.where(listed < SIDE, BOX, 0)
            factors = [scaled[kind, part, pl.ds(atom, 1), :] for part in range(2)]
            added = []
            for plane in range(PLANES):
                index = table_row(depth, plane, kind)
                for half in range(2):
                    weights = table_ref[index, half * 8 : half * 8 + 8, :]
                    for part in range(2):
                        values = weights * factors[part]
                        values = values + pltpu.roll(values, 64, 1)
                        values = values + pltpu.roll(values, 32, 1)
                        values = values + pltpu.roll(values, 16, 1)
                        values = jnp.where(inside, pltpu.roll(values, start_z, 1), 0.0)
                        added.append((part * PLANES + plane, start_y + half * 8, values))
            for where, start, values in added:
                padded[where, pl.ds(start, 8), :] = padded[where, pl.ds(start, 8), :] + values
        return carry

    lax.fori_loop(0, (listed_ref[SIDE + GROUP] + (GROUP - 1)) // GROUP, group_step, 0)
    for index in range(2 * PLANES):
        out_ref[index, 0:BOX, :] = padded[index, 0:BOX, :] + padded[index, SIDE:PAD, :]
        out_ref[index, BOX:SIDE, :] = padded[index, BOX:SIDE, :]


def local_kernel(wave_ref, potential_ref, wide_ref, out_ref):
    wide = wide_ref[...]
    pair = wide_ref[0:SIDE, :]
    for index in range(2 * PLANES):
        value = wave_ref[index]
        out_ref[index] = times_right(value, wide) + times_left(pair, value) + potential_ref[index % PLANES] * value


def depth_kernel(value_ref, wide_ref, out_ref):
    pair = wide_ref[0:SIDE, :]
    for row in range(8):
        out_ref[:, row, :] = times_left(pair, value_ref[:, row, :])


def final_kernel(local_ref, depth_ref, out_ref):
    half_step = 0.5 * time_step
    for plane in range(PLANES):
        out_ref[0, plane] = half_step * (local_ref[1, plane] + depth_ref[1, :, plane])
        out_ref[1, plane] = -half_step * (local_ref[0, plane] + depth_ref[0, :, plane])


def whole_step(wave, potential, occupations, centres, species, projectors, coupling):
    vmem, smem = whole(), whole(pltpu.SMEM)
    wide = kinetic_halves(SIDE)
    blocks = SIDE // 8
    first_plane = jnp.reshape(lax.axis_index("grid") * PLANES, (1,)).astype(jnp.int32)
    tiles = wave.reshape(2, PLANES, blocks, 8, SIDE)
    planes = wave.reshape(2 * PLANES, SIDE, SIDE)
    table_in = projectors.reshape(2 * BOX, NPROJ, BOX * BOX)

    sent = jnp.transpose(tiles, (0, 2, 1, 3, 4)).reshape(2 * blocks, PLANES, 8, SIDE)
    columns = lax.all_to_all(sent, "grid", 0, 0, tiled=True)

    terms = call(density_kernel, shape(2, 2, 2, PLANES, 16, SIDE), [smem, vmem])(
        occupations, wave.reshape(2, PLANES, SIDE, SIDE)
    )
    coef, table, listed = call(
        project_kernel,
        (shape(2 * NPROJ, SIDE), shape(2 * BOX + 1, BOX, SIDE), jax.ShapeDtypeStruct((SIDE + GROUP + 1,), jnp.int32)),
        [smem, smem, smem, vmem, vmem],
        [pltpu.VMEM((2 * PLANES, PAD, SIDE), F32), pltpu.VMEM((2, SIDE + 8, SIDE), F32)],
        outs=(vmem, vmem, smem),
    )(first_plane, centres, species, planes, table_in)
    coef = coef + permuted(coef, "grid", lambda place: place ^ 1)
    coef = coef + permuted(coef, "grid", lambda place: place ^ 2)
    above = permuted(coef, "grid", lambda place: place + 4)
    below = permuted(coef, "grid", lambda place: place - 4)
    total_coef = coef + above + below

    local = call(local_kernel, shape(2 * PLANES, SIDE, SIDE), [vmem] * 3)(planes, potential, wide)

    place = lax.axis_index("orb")
    for bit in (2, 4, 1):
        mine = (place // bit) % 2
        kept = lax.dynamic_index_in_dim(terms, mine, 0, keepdims=False)
        given = lax.dynamic_index_in_dim(terms, 1 - mine, 0, keepdims=False)
        terms = kept + permuted(given, "orb", lambda source: source ^ bit)
    density = terms

    depth = call(depth_kernel, shape(SIDE, 8, SIDE), [vmem] * 2)(
        columns.reshape(SIDE, 8, SIDE), wide
    )
    returned = lax.all_to_all(depth.reshape(2 * blocks, PLANES, 8, SIDE), "grid", 0, 0, tiled=True)

    total = call(
        spread_kernel,
        shape(2 * PLANES, SIDE, SIDE),
        [smem, smem, smem, smem, vmem, vmem, vmem, vmem],
        [pltpu.VMEM((2 * PLANES, PAD, SIDE), F32), pltpu.VMEM((2, 2, SIDE, SIDE), F32)],
    )(first_plane, centres, species, listed, total_coef, coupling, table, local)
    update = call(final_kernel, shape(2, PLANES, blocks, 8, SIDE), [vmem] * 2)(
        total.reshape(2, PLANES, blocks, 8, SIDE), returned.reshape(2, blocks, PLANES, 8, SIDE)
    )
    return (update.reshape(wave.shape), density)


def solution(mesh):
    placed = (
        P(None, "orb", "grid", None, None),
        P("grid", None, None),
        P("orb"),
        P(),
        P(),
        P(),
        P(),
    )
    return jax.shard_map(
        whole_step,
        mesh=mesh,
        in_specs=placed,
        out_specs=(P(None, "orb", "grid", None, None), P("grid", "orb", None)),
        check_vma=False,
    )
```

profile of v0, /device:TPU:8, one launch (start us, length us, event | category | flops | bytes accessed | tf_op | source)
XLA Modules:
  0.0 69.2 jit_solution(10960257421939268823)
XLA Ops:
  0.6 1.9 %copy.10 = f32[2,16,4,8,128]{4,3,2,1,0:T(8,128)} copy(f32[2,16,4,8,128]{4,3,1,2,0:T(8,128)} %bitcast.27) | data formatting | bytes 1048576 | tf_op jit(solution)/shard_map/transpose | solution.py:270
  2.5 11.4 %all-to-all-start = ((f32[32,4,8,128]{3,2,1,0:T(8,128)}), f32[32,4,8,128]{3,2,1,0:T(8,128)S(1)}, u32[]{:S(2)}, u32[]{:S(2)}) async-start(f32[32,4,8,128]{3,2,1,0:T(8,128)} %bitcast.6), calls=%async_computation | async-start | bytes 1048576 | tf_op jit(solution)/shard_map/all_to_all | solution.py:271
  14.7 0.0 copy-start.1
  14.8 0.5 collective-permute-start.4
  15.3 16.4 %all-to-all-done = f32[32,4,8,128]{3,2,1,0:T(8,128)S(1)} async-done(((f32[32,4,8,128]{3,2,1,0:T(8,128)}), f32[32,4,8,128]{3,2,1,0:T(8,128)S(1)}, u32[]{:S(2)}, u32[]{:S(2)}) %all-to-all-start) | async-done | bytes 524320 | tf_op jit(solution)/shard_map/all_to_all | solution.py:271
  31.7 2.5 %shard_map.98 = f32[128,8,128]{2,1,0:T(8,128)} custom-call(f32[128,8,128]{2,1,0:T(8,128)S(1)} %bitcast.32, bf16[256,256]{1,0:T(8,128)(2,1)S(1)} %copy-done.1), custom_call_target="tpu_custom_call" | custom-call | flops 1000000 | bytes 1000000 | tf_op jit(solution)/shard_map/pallas_call | solution.py:299
  34.2 4.9 %all-to-all-start.1 = ((f32[32,4,8,128]{3,2,1,0:T(8,128)}), f32[32,4,8,128]{3,2,1,0:T(8,128)S(1)}, u32[]{:S(2)}, u32[]{:S(2)}) async-start(f32[32,4,8,128]{3,2,1,0:T(8,128)} %bitcast.8), calls=%async_computation.1 | async-start | bytes 1048576 | tf_op jit(solution)/shard_map/all_to_all | solution.py:302
  39.1 0.0 copy-start.2
  39.2 2.4 %collective-permute-start.5 = (f32[2,4,16,128]{3,2,1,0:T(8,128)S(1)}, f32[2,4,16,128]{3,2,1,0:T(8,128)S(1)}, u32[]{:S(2)}, u32[]{:S(2)}) collective-permute-start(f32[2,4,16,128]{3,2,1,0:T(8,128)S(1)} %dynamic-slice_bitcast_fusion.1), channel_id=1, source_target_pairs={{0,4},{1,5},{2,6},{3,7},{4,0},{5,1},{6,2},{7,3},{8,12},{9,13},{10,... | collective-permute-start | bytes 196616 | tf_op jit(solution)/shard_map/ppermute | solution.py:28
  41.6 0.7 copy-done.5
  42.3 6.4 %shard_map.95 = (f32[16,128]{1,0:T(8,128)S(1)}, f32[33,16,128]{2,1,0:T(8,128)S(1)}, s32[133]{0:T(256)S(1)}) custom-call(s32[1]{0:T(128)} %bitcast.first_ref, s32[3,128]{1,0:T(4,128)S(1)} %copy-done.5, s32[128]{0:T(128)S(1)} %copy-done.6, f32[8,128,128]{2,1,0:T(8,128)S(1)} %bitcast.29, f32[32,8,256]{2,1,0:T(8,128)S(1)} %bitcast.34), custom_call_target="tpu_custom_call" | custom-call | flops 1000000 | bytes 1000000 | tf_op jit(solution)/shard_map/pallas_call | solution.py:276
  48.7 0.1 collective-permute-start
  48.8 1.2 %collective-permute-done = f32[16,128]{1,0:T(8,128)S(1)} collective-permute-done((f32[16,128]{1,0:T(8,128)S(1)}, f32[16,128]{1,0:T(8,128)S(1)}, u32[]{:S(2)}, u32[]{:S(2)}) %collective-permute-start) | collective-permute-done | bytes 8224 | tf_op jit(solution)/shard_map/ppermute | solution.py:28
  50.0 2.8 %collective-permute-start.1 = (f32[16,128]{1,0:T(8,128)S(1)}, f32[16,128]{1,0:T(8,128)S(1)}, u32[]{:S(2)}, u32[]{:S(2)}) collective-permute-start(f32[16,128]{1,0:T(8,128)S(1)} %add.58), channel_id=1, source_target_pairs={{0,16},{8,24},{16,0},{24,8},{32,48},{40,56},{48,32},{56,40},{64,80... | collective-permute-start | bytes 24584 | tf_op jit(solution)/shard_map/ppermute | solution.py:28
  52.8 0.4 shard_map.96.local_ref
  53.2 2.0 %collective-permute-done.1 = f32[16,128]{1,0:T(8,128)S(1)} collective-permute-done((f32[16,128]{1,0:T(8,128)S(1)}, f32[16,128]{1,0:T(8,128)S(1)}, u32[]{:S(2)}, u32[]{:S(2)}) %collective-permute-start.1) | collective-permute-done | bytes 8224 | tf_op jit(solution)/shard_map/ppermute | solution.py:28
  55.2 2.5 %collective-permute-start.3 = (f32[16,128]{1,0:T(8,128)S(1)}, f32[16,128]{1,0:T(8,128)S(1)}, u32[]{:S(2)}, u32[]{:S(2)}) collective-permute-start(f32[16,128]{1,0:T(8,128)S(1)} %add.59), channel_id=1, source_target_pairs={{0,224},{8,232},{16,240},{24,248},{32,0},{40,8},{48,16},{56,24},{6... | collective-permute-start | bytes 24584 | tf_op jit(solution)/shard_map/ppermute | solution.py:28
  57.8 0.0 copy-start.4
  57.8 0.7 collective-permute-start.6
  58.5 0.6 collective-permute-done.3
  59.1 3.5 %collective-permute-done.2 = f32[16,128]{1,0:T(8,128)S(1)} collective-permute-done((f32[16,128]{1,0:T(8,128)S(1)}, f32[16,128]{1,0:T(8,128)S(1)}, u32[]{:S(2)}, u32[]{:S(2)}) %collective-permute-start.2) | collective-permute-done | bytes 8224 | tf_op jit(solution)/shard_map/ppermute | solution.py:28
  62.6 5.0 %shard_map.97 = f32[8,128,128]{2,1,0:T(8,128)S(1)} custom-call(s32[1]{0:T(128)} %bitcast.first_ref, s32[3,128]{1,0:T(4,128)S(1)} %copy-done.5, s32[128]{0:T(128)S(1)} %copy-done.6, s32[133]{0:T(256)S(1)} %get-tuple-element.5.listed_ref, f32[16,128]{1,0:T(8,128)S(1)} %add_add_fusion.coef_ref, f32[2,8,8]{2,1,0:T(8,128)S(1)} %copy-done.4, ...), custom_call_target="tpu_custom_call" | custom-call | flops 1000000 | bytes 1000000 | tf_op jit(solution)/shard_map/pallas_call | solution.py:304
  67.7 0.6 bitcast_add_fusion.2
  68.3 0.9 %shard_map.99 = f32[2,4,16,8,128]{4,3,2,1,0:T(8,128)} custom-call(f32[2,4,16,8,128]{4,3,2,1,0:T(8,128)S(1)} %bitcast.33, f32[2,16,4,8,128]{4,3,2,1,0:T(8,128)S(1)} %bitcast.31), custom_call_target="tpu_custom_call" | custom-call | flops 1000000 | bytes 1000000 | tf_op jit(solution)/shard_map/pallas_call | solution.py:310
  (24 shorter events, 0.2 us)
Async XLA Ops:
  2.5 12.1 %copy-start = (f32[2,1,4,128,128]{4,3,2,1,0:T(8,128)S(1)}, f32[2,1,4,128,128]{4,3,2,1,0:T(8,128)}, u32[]{:S(2)}) copy-start(f32[2,1,4,128,128]{4,3,2,1,0:T(8,128)} %param.8) | copy-start | bytes 1572868
  2.5 29.2 %all-to-all-start = ((f32[32,4,8,128]{3,2,1,0:T(8,128)}), f32[32,4,8,128]{3,2,1,0:T(8,128)S(1)}, u32[]{:S(2)}, u32[]{:S(2)}) async-start(f32[32,4,8,128]{3,2,1,0:T(8,128)} %bitcast.6), calls=%async_computation | async-start | bytes 1048576 | tf_op jit(solution)/shard_map/all_to_all | solution.py:271
  14.7 17.0 %copy-start.1 = (bf16[256,256]{1,0:T(8,128)(2,1)S(1)}, bf16[256,256]{1,0:T(8,128)(2,1)}, u32[]{:S(2)}) copy-start(bf16[256,256]{1,0:T(8,128)(2,1)} %constant.84.clone.wide_ref) | copy-start | bytes 393220
  14.8 24.4 %collective-permute-start.4 = (f32[2,2,4,16,128]{4,3,2,1,0:T(8,128)S(1)}, f32[2,2,4,16,128]{4,3,2,1,0:T(8,128)S(1)}, u32[]{:S(2)}, u32[]{:S(2)}) collective-permute-start(f32[2,2,4,16,128]{4,3,2,1,0:T(8,128)S(1)} %dynamic-slice_bitcast_fusion), channel_id=1, source_target_pairs={{0,2},{1,3},{2,0},{3,1},{4,6},{5,7},{6,4},{7,5},{8,10},{9,11},{10,... | collective-permute-start | bytes 393224 | tf_op jit(solution)/shard_map/ppermute | solution.py:28
  34.2 34.1 %all-to-all-start.1 = ((f32[32,4,8,128]{3,2,1,0:T(8,128)}), f32[32,4,8,128]{3,2,1,0:T(8,128)S(1)}, u32[]{:S(2)}, u32[]{:S(2)}) async-start(f32[32,4,8,128]{3,2,1,0:T(8,128)} %bitcast.8), calls=%async_computation.1 | async-start | bytes 1048576 | tf_op jit(solution)/shard_map/all_to_all | solution.py:302
  39.1 2.5 %copy-start.2 = (f32[2,16,8,256]{3,2,1,0:T(8,128)S(1)}, f32[2,16,8,256]{3,2,1,0:T(8,128)}, u32[]{:S(2)}) copy-start(f32[2,16,8,256]{3,2,1,0:T(8,128)} %param.13) | copy-start | bytes 786436
  39.2 18.6 %collective-permute-start.5 = (f32[2,4,16,128]{3,2,1,0:T(8,128)S(1)}, f32[2,4,16,128]{3,2,1,0:T(8,128)S(1)}, u32[]{:S(2)}, u32[]{:S(2)}) collective-permute-start(f32[2,4,16,128]{3,2,1,0:T(8,128)S(1)} %dynamic-slice_bitcast_fusion.1), channel_id=1, source_target_pairs={{0,4},{1,5},{2,6},{3,7},{4,0},{5,1},{6,2},{7,3},{8,12},{9,13},{10,... | collective-permute-start | bytes 196616 | tf_op jit(solution)/shard_map/ppermute | solution.py:28
  41.6 0.7 copy-start.5
  41.6 0.7 copy-start.6
  42.3 10.5 %copy-start.3 = (f32[4,128,128]{2,1,0:T(8,128)S(1)}, f32[4,128,128]{2,1,0:T(8,128)}, u32[]{:S(2)}) copy-start(f32[4,128,128]{2,1,0:T(8,128)} %potential_ref.1) | copy-start | bytes 786436
  48.7 1.3 %collective-permute-start = (f32[16,128]{1,0:T(8,128)S(1)}, f32[16,128]{1,0:T(8,128)S(1)}, u32[]{:S(2)}, u32[]{:S(2)}) collective-permute-start(f32[16,128]{1,0:T(8,128)S(1)} %get-tuple-element.6), channel_id=1, source_target_pairs={{0,8},{8,0},{16,24},{24,16},{32,40},{40,32},{48,56},{56,48},{64,72... | collective-permute-start | bytes 24584 | tf_op jit(solution)/shard_map/ppermute | solution.py:28
  50.0 5.2 %collective-permute-start.1 = (f32[16,128]{1,0:T(8,128)S(1)}, f32[16,128]{1,0:T(8,128)S(1)}, u32[]{:S(2)}, u32[]{:S(2)}) collective-permute-start(f32[16,128]{1,0:T(8,128)S(1)} %add.58), channel_id=1, source_target_pairs={{0,16},{8,24},{16,0},{24,8},{32,48},{40,56},{48,32},{56,40},{64,80... | collective-permute-start | bytes 24584 | tf_op jit(solution)/shard_map/ppermute | solution.py:28
  55.2 3.9 %collective-permute-start.3 = (f32[16,128]{1,0:T(8,128)S(1)}, f32[16,128]{1,0:T(8,128)S(1)}, u32[]{:S(2)}, u32[]{:S(2)}) collective-permute-start(f32[16,128]{1,0:T(8,128)S(1)} %add.59), channel_id=1, source_target_pairs={{0,224},{8,232},{16,240},{24,248},{32,0},{40,8},{48,16},{56,24},{6... | collective-permute-start | bytes 24584 | tf_op jit(solution)/shard_map/ppermute | solution.py:28
  57.8 4.9 %collective-permute-start.2 = (f32[16,128]{1,0:T(8,128)S(1)}, f32[16,128]{1,0:T(8,128)S(1)}, u32[]{:S(2)}, u32[]{:S(2)}) collective-permute-start(f32[16,128]{1,0:T(8,128)S(1)} %add.59), channel_id=1, source_target_pairs={{0,32},{8,40},{16,48},{24,56},{32,64},{40,72},{48,80},{56,88},{64,... | collective-permute-start | bytes 24584 | tf_op jit(solution)/shard_map/ppermute | solution.py:28
  57.8 4.8 %copy-start.4 = (f32[2,8,8]{2,1,0:T(8,128)S(1)}, f32[2,8,8]{2,1,0:T(8,128)}, u32[]{:S(2)}) copy-start(f32[2,8,8]{2,1,0:T(8,128)} %coupling_ref.1) | copy-start | bytes 1540
  57.8 9.8 %collective-permute-start.6 = (f32[4,16,128]{2,1,0:T(8,128)S(1)}, f32[4,16,128]{2,1,0:T(8,128)S(1)}, u32[]{:S(2)}, u32[]{:S(2)}) collective-permute-start(f32[4,16,128]{2,1,0:T(8,128)S(1)} %dynamic-slice_bitcast_fusion.2), channel_id=1, source_target_pairs={{0,1},{1,0},{2,3},{3,2},{4,5},{5,4},{6,7},{7,6},{8,9},{9,8},{10,11... | collective-permute-start | bytes 98312 | tf_op jit(solution)/shard_map/ppermute | solution.py:28
where the time goes:
time: 69.5 us; the launch traced here: 69.2 us
  starting transfers between devices  25.4 us (37%)
  waiting for transfers between devices  23.7 us (34%)
  Pallas kernels  15.3 us (22%)
  local copies, waits for them, and re-layouts  2.65 us (4%)
  between operations  1.46 us (2%)
    all_to_all x1, waiting for transfers between devices, whole_step(): columns = lax.all_to_all(sent, 'grid', 0, 0, tiled=True)  16.4 us
    all_to_all x1, starting transfers between devices, whole_step(): columns = lax.all_to_all(sent, 'grid', 0, 0, tiled=True)  11.4 us
    ppermute x7, starting transfers between devices, permuted(): lax.ppermute(value, axis, [(source, target(source) % count) for source in...  8.99 us
    ppermute x7, waiting for transfers between devices, permuted(): lax.ppermute(value, axis, [(source, target(source) % count) for source in...  7.29 us
    pallas_call x1, Pallas kernels, whole_step(): call(project_kernel, (shape(2 * NPROJ, SIDE), shape(2 * BOX + 1, BOX, SID...  6.45 us
    pallas_call x1, Pallas kernels, whole_step(): call(spread_kernel, shape(2 * PLANES, SIDE, SIDE), [smem, smem, smem, sme...  5.02 us
    all_to_all x1, starting transfers between devices, whole_step(): lax.all_to_all(depth.reshape(2 * blocks, PLANES, 8, SIDE), 'grid', 0, 0,...  4.92 us
    pallas_call x1, Pallas kernels, whole_step(): call(depth_kernel, shape(SIDE, 8, SIDE), [vmem] * 2)  2.49 us
  transfers between devices with their start and end apart: 9, of which 5 were waited for; matrix products, arithmetic and copies ran while one was open for 1% of the time, Pallas kernels for 21%

commit v1 on v0

--- a/solution.py
+++ b/solution.py
@@ -163,17 +163,18 @@
         return carry
 
     lax.fori_loop(0, (count + (GROUP - 1)) // GROUP, group_step, 0)
-    group_row = lax.broadcasted_iota(jnp.int32, (NPROJ, SIDE), 0)
-    group_lane = lax.broadcasted_iota(jnp.int32, (NPROJ, SIDE), 1)
-    groups = (group_lane >> 4 == group_row).astype(F32)
-    for part in range(2):
-        coef_ref[part * 8 : part * 8 + 8, :] = lax.dot_general(
-            groups,
-            sums[part, 0:SIDE, :],
-            (((1,), (1,)), ((), ())),
-            precision=highest,
-            preferred_element_type=F32,
-        )
+    groups = ((lax.broadcasted_iota(jnp.int32, (NPROJ, 2 * SIDE), 1) >> 4) & (NPROJ - 1)) == (
+        lax.broadcasted_iota(jnp.int32, (NPROJ, 2 * SIDE), 0)
+    )
+    rows = jnp.concatenate([sums[part, 0:SIDE, :] for part in range(2)], axis=0)
+    coef = lax.dot_general(
+        groups.astype(F32).astype(BF16),
+        jnp.concatenate(halves(rows), axis=1),
+        (((1,), (1,)), ((), ())),
+        preferred_element_type=F32,
+    )
+    coef_ref[0:8, :] = coef[:, :SIDE]
+    coef_ref[8:16, :] = coef[:, SIDE:]
 
 
 def spread_kernel(
@@ -190,19 +191,23 @@
     scaled,
 ):
     lane = lax.broadcasted_iota(jnp.int32, (8, SIDE), 1)
-    groups = (lane >> 4 == lax.broadcasted_iota(jnp.int32, (8, SIDE), 0)).astype(F32)
-    for kind in range(2):
-        mixing = lax.dot_general(
-            coupling_ref[kind], groups, (((0,), (0,)), ((), ())), precision=highest, preferred_element_type=F32
-        )
-        for part in range(2):
-            scaled[kind, part] = lax.dot_general(
-                coef_ref[part * 8 : part * 8 + 8, :],
-                mixing,
-                (((0,), (0,)), ((), ())),
-                precision=highest,
-                preferred_element_type=F32,
-            )
+    groups = (lax.broadcasted_iota(jnp.int32, (2 * NPROJ, 2 * SIDE), 1) >> 4) == (
+        lax.broadcasted_iota(jnp.int32, (2 * NPROJ, 2 * SIDE), 0)
+    )
+    mixing = lax.dot_general(
+        coupling_ref[...],
+        groups.astype(F32),
+        (((0,), (0,)), ((), ())),
+        precision=highest,
+        preferred_element_type=F32,
+    )
+    scaled[...] = lax.dot_general(
+        jnp.concatenate([coef_ref[0:8, :], coef_ref[8:16, :]], axis=1),
+        mixing,
+        (((0,), (0,)), ((), ())),
+        precision=highest,
+        preferred_element_type=F32,
+    )
     for index in range(2 * PLANES):
         padded[index, 0:SIDE, :] = local_ref[index]
         padded[index, SIDE:PAD, :] = jnp.zeros((BOX, SIDE), F32)
@@ -214,7 +219,8 @@
             depth, start_y, start_z, _ = atom_place(first_ref, centres_ref, atom)
             kind = species_ref[atom]
             inside = ((lane - start_z) & (SIDE - 1)) < jnp.where(listed < SIDE, BOX, 0)
-            factors = [scaled[kind, part, pl.ds(atom, 1), :] for part in range(2)]
+            both = [scaled[pl.ds(part * SIDE + atom, 1), :] for part in range(2)]
+            factors = [jnp.where(kind == 0, pair[:, :SIDE], pair[:, SIDE:]) for pair in both]
             added = []
             for plane in range(PLANES):
                 index = table_row(depth, plane, kind)
@@ -305,8 +311,8 @@
         spread_kernel,
         shape(2 * PLANES, SIDE, SIDE),
         [smem, smem, smem, smem, vmem, vmem, vmem, vmem],
-        [pltpu.VMEM((2 * PLANES, PAD, SIDE), F32), pltpu.VMEM((2, 2, SIDE, SIDE), F32)],
-    )(first_plane, centres, species, listed, total_coef, coupling, table, local)
+        [pltpu.VMEM((2 * PLANES, PAD, SIDE), F32), pltpu.VMEM((2 * SIDE, 2 * SIDE), F32)],
+    )(first_plane, centres, species, listed, total_coef, coupling.reshape(2 * NPROJ, NPROJ), table, local)
     update = call(final_kernel, shape(2, PLANES, blocks, 8, SIDE), [vmem] * 2)(
         total.reshape(2, PLANES, blocks, 8, SIDE), returned.reshape(2, blocks, PLANES, 8, SIDE)
     )

time: 69.5 us -> 70.2 us (1.010)
  no operation moved by 1% of the time
where the time goes in v1:
time: 70.2 us; the launch traced here: 69.7 us
  starting transfers between devices  25.4 us (36%)
  waiting for transfers between devices  23.7 us (34%)
  Pallas kernels  15.2 us (22%)
  local copies, waits for them, and re-layouts  3.34 us (5%)
  between operations  1.46 us (2%)
    all_to_all x1, waiting for transfers between devices, whole_step(): columns = lax.all_to_all(sent, 'grid', 0, 0, tiled=True)  16.4 us
    all_to_all x1, starting transfers between devices, whole_step(): columns = lax.all_to_all(sent, 'grid', 0, 0, tiled=True)  11.4 us
    ppermute x7, starting transfers between devices, permuted(): lax.ppermute(value, axis, [(source, target(source) % count) for source in...  8.99 us
    ppermute x7, waiting for transfers between devices, permuted(): lax.ppermute(value, axis, [(source, target(source) % count) for source in...  7.31 us
    pallas_call x1, Pallas kernels, whole_step(): call(project_kernel, (shape(2 * NPROJ, SIDE), shape(2 * BOX + 1, BOX, SID...  6.45 us
    all_to_all x1, starting transfers between devices, whole_step(): lax.all_to_all(depth.reshape(2 * blocks, PLANES, 8, SIDE), 'grid', 0, 0,...  4.92 us
    pallas_call x1, Pallas kernels, whole_step(): call(spread_kernel, shape(2 * PLANES, SIDE, SIDE), [smem, smem, smem, sme...  4.9 us
    pallas_call x1, Pallas kernels, whole_step(): call(depth_kernel, shape(SIDE, 8, SIDE), [vmem] * 2)  2.49 us
  transfers between devices with their start and end apart: 9, of which 5 were waited for; matrix products, arithmetic and copies ran while one was open for 1% of the time, Pallas kernels for 21%

profile of v1, /device:TPU:8, one launch (start us, length us, event | category | flops | bytes accessed | tf_op | source)
XLA Modules:
  0.0 69.7 jit_solution(10331517410497096975)
XLA Ops:
  0.6 1.9 %copy.12 = f32[2,16,4,8,128]{4,3,2,1,0:T(8,128)} copy(f32[2,16,4,8,128]{4,3,1,2,0:T(8,128)} %bitcast.28) | data formatting | bytes 1048576 | tf_op jit(solution)/shard_map/transpose | solution.py:276
  2.5 11.4 %all-to-all-start = ((f32[32,4,8,128]{3,2,1,0:T(8,128)}), f32[32,4,8,128]{3,2,1,0:T(8,128)S(1)}, u32[]{:S(2)}, u32[]{:S(2)}) async-start(f32[32,4,8,128]{3,2,1,0:T(8,128)} %bitcast.7), calls=%async_computation | async-start | bytes 1048576 | tf_op jit(solution)/shard_map/all_to_all | solution.py:277
  14.7 0.0 copy-start.1
  14.8 0.5 collective-permute-start.4
  15.3 16.4 %all-to-all-done = f32[32,4,8,128]{3,2,1,0:T(8,128)S(1)} async-done(((f32[32,4,8,128]{3,2,1,0:T(8,128)}), f32[32,4,8,128]{3,2,1,0:T(8,128)S(1)}, u32[]{:S(2)}, u32[]{:S(2)}) %all-to-all-start) | async-done | bytes 524320 | tf_op jit(solution)/shard_map/all_to_all | solution.py:277
  31.7 2.5 %shard_map.98 = f32[128,8,128]{2,1,0:T(8,128)} custom-call(f32[128,8,128]{2,1,0:T(8,128)S(1)} %bitcast.33, bf16[256,256]{1,0:T(8,128)(2,1)S(1)} %copy-done.1), custom_call_target="tpu_custom_call" | custom-call | flops 1000000 | bytes 1000000 | tf_op jit(solution)/shard_map/pallas_call | solution.py:305
  34.2 4.9 %all-to-all-start.1 = ((f32[32,4,8,128]{3,2,1,0:T(8,128)}), f32[32,4,8,128]{3,2,1,0:T(8,128)S(1)}, u32[]{:S(2)}, u32[]{:S(2)}) async-start(f32[32,4,8,128]{3,2,1,0:T(8,128)} %bitcast.9), calls=%async_computation.1 | async-start | bytes 1048576 | tf_op jit(solution)/shard_map/all_to_all | solution.py:308
  39.1 0.0 copy-start.2
  39.2 2.4 %collective-permute-start.5 = (f32[2,4,16,128]{3,2,1,0:T(8,128)S(1)}, f32[2,4,16,128]{3,2,1,0:T(8,128)S(1)}, u32[]{:S(2)}, u32[]{:S(2)}) collective-permute-start(f32[2,4,16,128]{3,2,1,0:T(8,128)S(1)} %dynamic-slice_bitcast_fusion.1), channel_id=1, source_target_pairs={{0,4},{1,5},{2,6},{3,7},{4,0},{5,1},{6,2},{7,3},{8,12},{9,13},{10,... | collective-permute-start | bytes 196616 | tf_op jit(solution)/shard_map/ppermute | solution.py:28
  41.6 0.7 copy-done.5
  42.3 6.4 %shard_map.95 = (f32[16,128]{1,0:T(8,128)S(1)}, f32[33,16,128]{2,1,0:T(8,128)S(1)}, s32[133]{0:T(256)S(1)}) custom-call(s32[1]{0:T(128)} %bitcast.first_ref, s32[3,128]{1,0:T(4,128)S(1)} %copy-done.5, s32[128]{0:T(128)S(1)} %copy-done.6, f32[8,128,128]{2,1,0:T(8,128)S(1)} %bitcast.30, f32[32,8,256]{2,1,0:T(8,128)S(1)} %bitcast.35), custom_call_target="tpu_custom_call" | custom-call | flops 1000000 | bytes 1000000 | tf_op jit(solution)/shard_map/pallas_call | solution.py:282
  48.7 0.1 collective-permute-start
  48.8 1.2 %collective-permute-done = f32[16,128]{1,0:T(8,128)S(1)} collective-permute-done((f32[16,128]{1,0:T(8,128)S(1)}, f32[16,128]{1,0:T(8,128)S(1)}, u32[]{:S(2)}, u32[]{:S(2)}) %collective-permute-start) | collective-permute-done | bytes 8224 | tf_op jit(solution)/shard_map/ppermute | solution.py:28
  50.0 2.8 %collective-permute-start.1 = (f32[16,128]{1,0:T(8,128)S(1)}, f32[16,128]{1,0:T(8,128)S(1)}, u32[]{:S(2)}, u32[]{:S(2)}) collective-permute-start(f32[16,128]{1,0:T(8,128)S(1)} %add.58), channel_id=1, source_target_pairs={{0,16},{8,24},{16,0},{24,8},{32,48},{40,56},{48,32},{56,40},{64,80... | collective-permute-start | bytes 24584 | tf_op jit(solution)/shard_map/ppermute | solution.py:28
  52.8 0.4 shard_map.96.local_ref
  53.2 2.0 %collective-permute-done.1 = f32[16,128]{1,0:T(8,128)S(1)} collective-permute-done((f32[16,128]{1,0:T(8,128)S(1)}, f32[16,128]{1,0:T(8,128)S(1)}, u32[]{:S(2)}, u32[]{:S(2)}) %collective-permute-start.1) | collective-permute-done | bytes 8224 | tf_op jit(solution)/shard_map/ppermute | solution.py:28
  55.2 2.5 %collective-permute-start.3 = (f32[16,128]{1,0:T(8,128)S(1)}, f32[16,128]{1,0:T(8,128)S(1)}, u32[]{:S(2)}, u32[]{:S(2)}) collective-permute-start(f32[16,128]{1,0:T(8,128)S(1)} %add.59), channel_id=1, source_target_pairs={{0,224},{8,232},{16,240},{24,248},{32,0},{40,8},{48,16},{56,24},{6... | collective-permute-start | bytes 24584 | tf_op jit(solution)/shard_map/ppermute | solution.py:28
  57.8 0.7 collective-permute-start.6
  58.5 0.6 collective-permute-done.3
  59.1 3.5 %collective-permute-done.2 = f32[16,128]{1,0:T(8,128)S(1)} collective-permute-done((f32[16,128]{1,0:T(8,128)S(1)}, f32[16,128]{1,0:T(8,128)S(1)}, u32[]{:S(2)}, u32[]{:S(2)}) %collective-permute-start.2) | collective-permute-done | bytes 8224 | tf_op jit(solution)/shard_map/ppermute | solution.py:28
  62.6 0.7 copy-done.4
  63.3 4.9 %shard_map.97 = f32[8,128,128]{2,1,0:T(8,128)S(1)} custom-call(s32[1]{0:T(128)} %bitcast.first_ref, s32[3,128]{1,0:T(4,128)S(1)} %copy-done.5, s32[128]{0:T(128)S(1)} %copy-done.6, s32[133]{0:T(256)S(1)} %get-tuple-element.5.listed_ref, f32[16,128]{1,0:T(8,128)S(1)} %add_add_fusion.coef_ref, f32[16,8]{1,0:T(8,128)S(1)} %bitcast.36, ...), custom_call_target="tpu_custom_call" | custom-call | flops 1000000 | bytes 1000000 | tf_op jit(solution)/shard_map/pallas_call | solution.py:310
  68.2 0.6 bitcast_add_fusion.2
  68.9 0.9 %shard_map.99 = f32[2,4,16,8,128]{4,3,2,1,0:T(8,128)} custom-call(f32[2,4,16,8,128]{4,3,2,1,0:T(8,128)S(1)} %bitcast.34, f32[2,16,4,8,128]{4,3,2,1,0:T(8,128)S(1)} %bitcast.32), custom_call_target="tpu_custom_call" | custom-call | flops 1000000 | bytes 1000000 | tf_op jit(solution)/shard_map/pallas_call | solution.py:316
  (24 shorter events, 0.2 us)
Async XLA Ops:
  2.5 12.1 %copy-start = (f32[2,1,4,128,128]{4,3,2,1,0:T(8,128)S(1)}, f32[2,1,4,128,128]{4,3,2,1,0:T(8,128)}, u32[]{:S(2)}) copy-start(f32[2,1,4,128,128]{4,3,2,1,0:T(8,128)} %param.8) | copy-start | bytes 1572868
  2.5 29.2 %all-to-all-start = ((f32[32,4,8,128]{3,2,1,0:T(8,128)}), f32[32,4,8,128]{3,2,1,0:T(8,128)S(1)}, u32[]{:S(2)}, u32[]{:S(2)}) async-start(f32[32,4,8,128]{3,2,1,0:T(8,128)} %bitcast.7), calls=%async_computation | async-start | bytes 1048576 | tf_op jit(solution)/shard_map/all_to_all | solution.py:277
  14.7 17.0 %copy-start.1 = (bf16[256,256]{1,0:T(8,128)(2,1)S(1)}, bf16[256,256]{1,0:T(8,128)(2,1)}, u32[]{:S(2)}) copy-start(bf16[256,256]{1,0:T(8,128)(2,1)} %constant.84.clone.wide_ref) | copy-start | bytes 393220
  14.8 24.4 %collective-permute-start.4 = (f32[2,2,4,16,128]{4,3,2,1,0:T(8,128)S(1)}, f32[2,2,4,16,128]{4,3,2,1,0:T(8,128)S(1)}, u32[]{:S(2)}, u32[]{:S(2)}) collective-permute-start(f32[2,2,4,16,128]{4,3,2,1,0:T(8,128)S(1)} %dynamic-slice_bitcast_fusion), channel_id=1, source_target_pairs={{0,2},{1,3},{2,0},{3,1},{4,6},{5,7},{6,4},{7,5},{8,10},{9,11},{10,... | collective-permute-start | bytes 393224 | tf_op jit(solution)/shard_map/ppermute | solution.py:28
  34.2 34.7 %all-to-all-start.1 = ((f32[32,4,8,128]{3,2,1,0:T(8,128)}), f32[32,4,8,128]{3,2,1,0:T(8,128)S(1)}, u32[]{:S(2)}, u32[]{:S(2)}) async-start(f32[32,4,8,128]{3,2,1,0:T(8,128)} %bitcast.9), calls=%async_computation.1 | async-start | bytes 1048576 | tf_op jit(solution)/shard_map/all_to_all | solution.py:308
  39.1 2.5 %copy-start.2 = (f32[2,16,8,256]{3,2,1,0:T(8,128)S(1)}, f32[2,16,8,256]{3,2,1,0:T(8,128)}, u32[]{:S(2)}) copy-start(f32[2,16,8,256]{3,2,1,0:T(8,128)} %param.13) | copy-start | bytes 786436
  39.2 18.6 %collective-permute-start.5 = (f32[2,4,16,128]{3,2,1,0:T(8,128)S(1)}, f32[2,4,16,128]{3,2,1,0:T(8,128)S(1)}, u32[]{:S(2)}, u32[]{:S(2)}) collective-permute-start(f32[2,4,16,128]{3,2,1,0:T(8,128)S(1)} %dynamic-slice_bitcast_fusion.1), channel_id=1, source_target_pairs={{0,4},{1,5},{2,6},{3,7},{4,0},{5,1},{6,2},{7,3},{8,12},{9,13},{10,... | collective-permute-start | bytes 196616 | tf_op jit(solution)/shard_map/ppermute | solution.py:28
  41.6 0.7 copy-start.5
  41.6 0.7 copy-start.6
  42.3 10.5 %copy-start.3 = (f32[4,128,128]{2,1,0:T(8,128)S(1)}, f32[4,128,128]{2,1,0:T(8,128)}, u32[]{:S(2)}) copy-start(f32[4,128,128]{2,1,0:T(8,128)} %potential_ref.1) | copy-start | bytes 786436
  48.7 1.3 %collective-permute-start = (f32[16,128]{1,0:T(8,128)S(1)}, f32[16,128]{1,0:T(8,128)S(1)}, u32[]{:S(2)}, u32[]{:S(2)}) collective-permute-start(f32[16,128]{1,0:T(8,128)S(1)} %get-tuple-element.6), channel_id=1, source_target_pairs={{0,8},{8,0},{16,24},{24,16},{32,40},{40,32},{48,56},{56,48},{64,72... | collective-permute-start | bytes 24584 | tf_op jit(solution)/shard_map/ppermute | solution.py:28
  50.0 5.2 %collective-permute-start.1 = (f32[16,128]{1,0:T(8,128)S(1)}, f32[16,128]{1,0:T(8,128)S(1)}, u32[]{:S(2)}, u32[]{:S(2)}) collective-permute-start(f32[16,128]{1,0:T(8,128)S(1)} %add.58), channel_id=1, source_target_pairs={{0,16},{8,24},{16,0},{24,8},{32,48},{40,56},{48,32},{56,40},{64,80... | collective-permute-start | bytes 24584 | tf_op jit(solution)/shard_map/ppermute | solution.py:28
  55.2 3.9 %collective-permute-start.3 = (f32[16,128]{1,0:T(8,128)S(1)}, f32[16,128]{1,0:T(8,128)S(1)}, u32[]{:S(2)}, u32[]{:S(2)}) collective-permute-start(f32[16,128]{1,0:T(8,128)S(1)} %add.59), channel_id=1, source_target_pairs={{0,224},{8,232},{16,240},{24,248},{32,0},{40,8},{48,16},{56,24},{6... | collective-permute-start | bytes 24584 | tf_op jit(solution)/shard_map/ppermute | solution.py:28
  57.8 4.9 %collective-permute-start.2 = (f32[16,128]{1,0:T(8,128)S(1)}, f32[16,128]{1,0:T(8,128)S(1)}, u32[]{:S(2)}, u32[]{:S(2)}) collective-permute-start(f32[16,128]{1,0:T(8,128)S(1)} %add.59), channel_id=1, source_target_pairs={{0,32},{8,40},{16,48},{24,56},{32,64},{40,72},{48,80},{56,88},{64,... | collective-permute-start | bytes 24584 | tf_op jit(solution)/shard_map/ppermute | solution.py:28
  57.8 10.4 %collective-permute-start.6 = (f32[4,16,128]{2,1,0:T(8,128)S(1)}, f32[4,16,128]{2,1,0:T(8,128)S(1)}, u32[]{:S(2)}, u32[]{:S(2)}) collective-permute-start(f32[4,16,128]{2,1,0:T(8,128)S(1)} %dynamic-slice_bitcast_fusion.2), channel_id=1, source_target_pairs={{0,1},{1,0},{2,3},{3,2},{4,5},{5,4},{6,7},{7,6},{8,9},{9,8},{10,11... | collective-permute-start | bytes 98312 | tf_op jit(solution)/shard_map/ppermute | solution.py:28
  62.6 0.7 copy-start.4

commit v2 on v1

--- a/solution.py
+++ b/solution.py
@@ -19,6 +19,8 @@
 PLANES = 4
 PAD = SIDE + BOX
 GROUP = 4
+FIELD = 136
+COUNT = 5 * FIELD
 F32 = jnp.float32
 BF16 = jnp.bfloat16
 
@@ -102,8 +104,8 @@
     return tile
 
 
-def atom_place(first_ref, centres_ref, atom):
-    depth = (first_ref[0] - centres_ref[0, atom] + (BOX // 2 + SIDE)) & (SIDE - 1)
+def atom_place(first_plane, centres_ref, atom):
+    depth = (first_plane - centres_ref[0, atom] + (BOX // 2 + SIDE)) & (SIDE - 1)
     start_y = (centres_ref[1, atom] + (SIDE - BOX // 2)) & (SIDE - 1)
     start_z = (centres_ref[2, atom] + (SIDE - BOX // 2)) & (SIDE - 1)
     touched = ((depth + (PLANES - 1)) & (SIDE - 1)) < BOX + PLANES - 1
@@ -115,9 +117,15 @@
     return jnp.where(slot < BOX, kind * BOX + slot, 2 * BOX)
 
 
-def project_kernel(
-    first_ref, centres_ref, species_ref, wave_ref, projectors_ref, coef_ref, table_ref, listed_ref, padded, sums
-):
+def entry(listed_ref, index):
+    return [listed_ref[field * FIELD + index] for field in range(5)]
+
+
+def group_count(listed_ref):
+    return (listed_ref[COUNT] + (GROUP - 1)) // GROUP
+
+
+def project_kernel(listed_ref, wave_ref, projectors_ref, coef_ref, table_ref, padded, sums):
     lane = lax.broadcasted_iota(jnp.int32, (8, SIDE), 1)
     row = lax.broadcasted_iota(jnp.int32, (8, SIDE), 0)
     for index in range(2 * PLANES):
@@ -125,16 +133,6 @@
         padded[index, SIDE:PAD, :] = wave_ref[index, 0:BOX, :]
     sums[...] = jnp.zeros_like(sums)
 
-    def list_step(atom, count):
-        touched = atom_place(first_ref, centres_ref, atom)[3]
-        listed_ref[count] = atom
-        return count + touched.astype(jnp.int32)
-
-    count = lax.fori_loop(0, SIDE, list_step, 0, unroll=8)
-    listed_ref[SIDE + GROUP] = count
-    for extra in range(GROUP):
-        listed_ref[count + extra] = SIDE
-
     for index in range(2 * BOX):
         for half in range(2):
             tile = projectors_ref[index, :, half * SIDE : (half + 1) * SIDE]
@@ -144,10 +142,7 @@
 
     def group_step(step, carry):
         for offset in range(GROUP):
-            listed = listed_ref[step * GROUP + offset]
-            atom = jnp.minimum(listed, SIDE - 1)
-            depth, start_y, start_z, _ = atom_place(first_ref, centres_ref, atom)
-            kind = species_ref[atom]
+            listed, depth, start_y, start_z, kind = entry(listed_ref, step * GROUP + offset)
             picks = (inner + start_z) & (SIDE - 1)
             totals = [jnp.zeros((8, SIDE), F32), jnp.zeros((8, SIDE), F32)]
             for plane in range(PLANES):
@@ -162,7 +157,7 @@
                 sums[part, pl.ds(listed, 1), :] = jnp.sum(totals[part], axis=0, keepdims=True)
         return carry
 
-    lax.fori_loop(0, (count + (GROUP - 1)) // GROUP, group_step, 0)
+    lax.fori_loop(0, group_count(listed_ref), group_step, 0)
     groups = ((lax.broadcasted_iota(jnp.int32, (NPROJ, 2 * SIDE), 1) >> 4) & (NPROJ - 1)) == (
         lax.broadcasted_iota(jnp.int32, (NPROJ, 2 * SIDE), 0)
     )
@@ -178,9 +173,6 @@
 
 
 def spread_kernel(
-    first_ref,
-    centres_ref,
-    species_ref,
     listed_ref,
     coef_ref,
     coupling_ref,
@@ -214,11 +206,9 @@
 
     def group_step(step, carry):
         for offset in range(GROUP):
-            listed = listed_ref[step * GROUP + offset]
+            listed, depth, start_y, start_z, kind = entry(listed_ref, step * GROUP + offset)
             atom = jnp.minimum(listed, SIDE - 1)
-            depth, start_y, start_z, _ = atom_place(first_ref, centres_ref, atom)
-            kind = species_ref[atom]
-            inside = ((lane - start_z) & (SIDE - 1)) < jnp.where(listed < SIDE, BOX, 0)
+            inside = ((lane - start_z) & (SIDE - 1)) < BOX
             both = [scaled[pl.ds(part * SIDE + atom, 1), :] for part in range(2)]
             factors = [jnp.where(kind == 0, pair[:, :SIDE], pair[:, SIDE:]) for pair in both]
             added = []
@@ -237,7 +227,7 @@
                 padded[where, pl.ds(start, 8), :] = padded[where, pl.ds(start, 8), :] + values
         return carry
 
-    lax.fori_loop(0, (listed_ref[SIDE + GROUP] + (GROUP - 1)) // GROUP, group_step, 0)
+    lax.fori_loop(0, group_count(listed_ref), group_step, 0)
     for index in range(2 * PLANES):
         out_ref[index, 0:BOX, :] = padded[index, 0:BOX, :] + padded[index, SIDE:PAD, :]
         out_ref[index, BOX:SIDE, :] = padded[index, BOX:SIDE, :]
@@ -251,21 +241,97 @@
         out_ref[index] = times_right(value, wide) + times_left(pair, value) + potential_ref[index % PLANES] * value
 
 
-def depth_kernel(value_ref, wide_ref, out_ref):
+def depth_kernel(value_ref, wide_ref, out_ref, rows, sems):
     pair = wide_ref[0:SIDE, :]
+    copies = []
     for row in range(8):
-        out_ref[:, row, :] = times_left(pair, value_ref[:, row, :])
-
-
-def final_kernel(local_ref, depth_ref, out_ref):
+        rows[row] = times_left(pair, value_ref[pl.ds(row, SIDE, stride=8), :])
+        copies.append(pltpu.make_async_copy(rows.at[row], out_ref.at[:, row, :], sems.at[row]))
+        copies[-1].start()
+    for copy in copies:
+        copy.wait()
+
+
+def list_atoms(first_plane, centres_ref, species_ref, listed_ref):
+    def list_step(atom, count):
+        touched = atom_place(first_plane, centres_ref, atom)[3]
+        listed_ref[count] = atom
+        return count + touched.astype(jnp.int32)
+
+    count = lax.fori_loop(0, SIDE, list_step, 0, unroll=8)
+    listed_ref[COUNT] = count
+
+    def detail_step(index, carry):
+        atom = listed_ref[index]
+        depth, start_y, start_z, _ = atom_place(first_plane, centres_ref, atom)
+        for field, value in enumerate((depth, start_y, start_z, species_ref[atom])):
+            listed_ref[(field + 1) * FIELD + index] = value
+        return carry
+
+    lax.fori_loop(0, count, detail_step, 0)
+    for extra in range(GROUP):
+        for field, value in enumerate((SIDE, SIDE // 2, 0, 0, 0)):
+            listed_ref[field * FIELD + count + extra] = jnp.int32(value)
+
+
+def pack_kernel(
+    first_ref,
+    wave_ref,
+    centres_ref,
+    species_ref,
+    out_ref,
+    listed_out_ref,
+    held,
+    centres,
+    species,
+    listed,
+    in_sems,
+    out_sems,
+    list_sems,
+):
+    places = [(part, plane) for part in range(2) for plane in range(PLANES)]
+    arriving = [
+        pltpu.make_async_copy(wave_ref.at[place], held.at[place], in_sems.at[slot]) for slot, place in enumerate(places)
+    ]
+    leaving = [
+        pltpu.make_async_copy(held.at[part, plane], out_ref.at[part, :, plane], out_sems.at[slot])
+        for slot, (part, plane) in enumerate(places)
+    ]
+    tables = [
+        pltpu.make_async_copy(centres_ref, centres, list_sems.at[0]),
+        pltpu.make_async_copy(species_ref, species, list_sems.at[1]),
+    ]
+    listing = pltpu.make_async_copy(listed, listed_out_ref, list_sems.at[2])
+    for copy in tables + arriving:
+        copy.start()
+    for first, second in zip(arriving, leaving):
+        first.wait()
+        second.start()
+    for copy in tables:
+        copy.wait()
+    list_atoms(first_ref[0], centres, species, listed)
+    listing.start()
+    for copy in leaving:
+        copy.wait()
+    listing.wait()
+
+
+def final_kernel(local_ref, depth_ref, out_ref, held, sems):
     half_step = 0.5 * time_step
+    copies = []
     for plane in range(PLANES):
-        out_ref[0, plane] = half_step * (local_ref[1, plane] + depth_ref[1, :, plane])
-        out_ref[1, plane] = -half_step * (local_ref[0, plane] + depth_ref[0, :, plane])
+        for part, sign in ((0, half_step), (1, -half_step)):
+            held[part, plane] = sign * (local_ref[1 - part, plane] + depth_ref[1 - part, :, plane])
+            copies.append(
+                pltpu.make_async_copy(held.at[part, plane], out_ref.at[part, plane], sems.at[part * PLANES + plane])
+            )
+            copies[-1].start()
+    for copy in copies:
+        copy.wait()
 
 
 def whole_step(wave, potential, occupations, centres, species, projectors, coupling):
-    vmem, smem = whole(), whole(pltpu.SMEM)
+    vmem, smem, outside = whole(), whole(pltpu.SMEM), whole(pl.ANY)
     wide = kinetic_halves(SIDE)
     blocks = SIDE // 8
     first_plane = jnp.reshape(lax.axis_index("grid") * PLANES, (1,)).astype(jnp.int32)
@@ -273,19 +339,33 @@
     planes = wave.reshape(2 * PLANES, SIDE, SIDE)
     table_in = projectors.reshape(2 * BOX, NPROJ, BOX * BOX)
 
-    sent = jnp.transpose(tiles, (0, 2, 1, 3, 4)).reshape(2 * blocks, PLANES, 8, SIDE)
+    sent, listed = call(
+        pack_kernel,
+        (shape(2, blocks, PLANES, 8, SIDE), jax.ShapeDtypeStruct((COUNT + FIELD,), jnp.int32)),
+        [smem] + [whole(pltpu.HBM)] * 3,
+        [
+            pltpu.VMEM((2, PLANES, blocks, 8, SIDE), F32),
+            pltpu.SMEM((3, SIDE), jnp.int32),
+            pltpu.SMEM((SIDE,), jnp.int32),
+            pltpu.SMEM((COUNT + FIELD,), jnp.int32),
+            pltpu.SemaphoreType.DMA((2 * PLANES,)),
+            pltpu.SemaphoreType.DMA((2 * PLANES,)),
+            pltpu.SemaphoreType.DMA((3,)),
+        ],
+        outs=(outside, outside),
+    )(first_plane, *(pltpu.with_memory_space_constraint(value, pltpu.HBM) for value in (tiles, centres, species)))
+    sent = sent.reshape(2 * blocks, PLANES, 8, SIDE)
     columns = lax.all_to_all(sent, "grid", 0, 0, tiled=True)
 
     terms = call(density_kernel, shape(2, 2, 2, PLANES, 16, SIDE), [smem, vmem])(
         occupations, wave.reshape(2, PLANES, SIDE, SIDE)
     )
-    coef, table, listed = call(
+    coef, table = call(
         project_kernel,
-        (shape(2 * NPROJ, SIDE), shape(2 * BOX + 1, BOX, SIDE), jax.ShapeDtypeStruct((SIDE + GROUP + 1,), jnp.int32)),
-        [smem, smem, smem, vmem, vmem],
+        (shape(2 * NPROJ, SIDE), shape(2 * BOX + 1, BOX, SIDE)),
+        [smem, vmem, vmem],
         [pltpu.VMEM((2 * PLANES, PAD, SIDE), F32), pltpu.VMEM((2, SIDE + 8, SIDE), F32)],
-        outs=(vmem, vmem, smem),
-    )(first_plane, centres, species, planes, table_in)
+    )(listed, planes, table_in)
     coef = coef + permuted(coef, "grid", lambda place: place ^ 1)
     coef = coef + permuted(coef, "grid", lambda place: place ^ 2)
     above = permuted(coef, "grid", lambda place: place + 4)
@@ -302,18 +382,28 @@
         terms = kept + permuted(given, "orb", lambda source: source ^ bit)
     density = terms
 
-    depth = call(depth_kernel, shape(SIDE, 8, SIDE), [vmem] * 2)(
-        columns.reshape(SIDE, 8, SIDE), wide
-    )
+    depth = call(
+        depth_kernel,
+        shape(SIDE, 8, SIDE),
+        [vmem] * 2,
+        [pltpu.VMEM((8, SIDE, SIDE), F32), pltpu.SemaphoreType.DMA((8,))],
+        outs=outside,
+    )(columns.reshape(8 * SIDE, SIDE), wide)
     returned = lax.all_to_all(depth.reshape(2 * blocks, PLANES, 8, SIDE), "grid", 0, 0, tiled=True)
 
     total = call(
         spread_kernel,
         shape(2 * PLANES, SIDE, SIDE),
-        [smem, smem, smem, smem, vmem, vmem, vmem, vmem],
+        [smem, vmem, vmem, vmem, vmem],
         [pltpu.VMEM((2 * PLANES, PAD, SIDE), F32), pltpu.VMEM((2 * SIDE, 2 * SIDE), F32)],
-    )(first_plane, centres, species, listed, total_coef, coupling.reshape(2 * NPROJ, NPROJ), table, local)
-    update = call(final_kernel, shape(2, PLANES, blocks, 8, SIDE), [vmem] * 2)(
+    )(listed, total_coef, coupling.reshape(2 * NPROJ, NPROJ), table, local)
+    update = call(
+        final_kernel,
+        shape(2, PLANES, blocks, 8, SIDE),
+        [vmem] * 2,
+        [pltpu.VMEM((2, PLANES, blocks, 8, SIDE), F32), pltpu.SemaphoreType.DMA((2 * PLANES,))],
+        outs=outside,
+    )(
         total.reshape(2, PLANES, blocks, 8, SIDE), returned.reshape(2, blocks, PLANES, 8, SIDE)
     )
     return (update.reshape(wave.shape), density)

time: 70.2 us -> 66.9 us (0.953)
  the two profiles are of different devices: /device:TPU:8 before, /device:TPU:1 now
where the time goes in v2:
time: 66.9 us; the launch traced here: 65.8 us
  starting transfers between devices  28.6 us (43%)
  waiting for transfers between devices  20.2 us (30%)
  Pallas kernels  14.7 us (22%)
  between operations  1.48 us (2%)
  other arithmetic  0.67 us (1%)
    all_to_all x1, waiting for transfers between devices, whole_step(): columns = lax.all_to_all(sent, 'grid', 0, 0, tiled=True)  14.7 us
    all_to_all x1, starting transfers between devices, whole_step(): columns = lax.all_to_all(sent, 'grid', 0, 0, tiled=True)  12.6 us
    ppermute x7, starting transfers between devices, permuted(): lax.ppermute(value, axis, [(source, target(source) % count) for source in...  10.2 us
    all_to_all x1, starting transfers between devices, whole_step(): lax.all_to_all(depth.reshape(2 * blocks, PLANES, 8, SIDE), 'grid', 0, 0,...  5.83 us
    ppermute x7, waiting for transfers between devices, permuted(): lax.ppermute(value, axis, [(source, target(source) % count) for source in...  5.55 us
    pallas_call x1, Pallas kernels, whole_step(): call(project_kernel, (shape(2 * NPROJ, SIDE), shape(2 * BOX + 1, BOX, SID...  5.27 us
    pallas_call x1, Pallas kernels, whole_step(): call(spread_kernel, shape(2 * PLANES, SIDE, SIDE), [smem, vmem, vmem, vme...  4.34 us
    pallas_call x1, Pallas kernels, whole_step(): call(pack_kernel, (shape(2, blocks, PLANES, 8, SIDE), jax.ShapeDtypeStruc...  2.65 us
  transfers between devices with their start and end apart: 9, of which 5 were waited for; matrix products, arithmetic and copies ran while one was open for 1% of the time, Pallas kernels for 17%

profile of v2, /device:TPU:1, one launch (start us, length us, event | category | flops | bytes accessed | tf_op | source)
XLA Modules:
  0.0 65.8 jit_solution(15208870298891644116)
XLA Ops:
  0.6 2.6 %shard_map.95 = (f32[2,16,4,8,128]{4,3,2,1,0:T(8,128)}, s32[816]{0:T(1024)S(1)}) custom-call(s32[1]{0:T(128)} %bitcast.first_ref, f32[2,4,16,8,128]{4,3,2,1,0:T(8,128)} %bitcast.26, s32[3,128]{1,0:T(4,128)} %centres_ref.1, s32[128]{0:T(128)} %species_ref.1), custom_call_target="tpu_custom_call" | custom-call | flops 1000000 | bytes 1000000 | tf_op jit(solution)/shard_map/pallas_call | solution.py:342
  3.3 0.0 copy-start
  3.3 12.6 %all-to-all-start = ((f32[32,4,8,128]{3,2,1,0:T(8,128)}), f32[32,4,8,128]{3,2,1,0:T(8,128)S(1)}, u32[]{:S(2)}, u32[]{:S(2)}) async-start(f32[32,4,8,128]{3,2,1,0:T(8,128)} %bitcast.6), calls=%async_computation | async-start | bytes 1048576 | tf_op jit(solution)/shard_map/all_to_all | solution.py:358
  16.7 0.0 copy-start.1
  16.7 1.4 %collective-permute-start.4 = (f32[2,2,4,16,128]{4,3,2,1,0:T(8,128)S(1)}, f32[2,2,4,16,128]{4,3,2,1,0:T(8,128)S(1)}, u32[]{:S(2)}, u32[]{:S(2)}) collective-permute-start(f32[2,2,4,16,128]{4,3,2,1,0:T(8,128)S(1)} %dynamic-slice_bitcast_fusion), channel_id=1, source_target_pairs={{0,2},{1,3},{2,0},{3,1},{4,6},{5,7},{6,4},{7,5},{8,10},{9,11},{10,... | collective-permute-start | bytes 393224 | tf_op jit(solution)/shard_map/ppermute | solution.py:30
  18.1 14.7 %all-to-all-done = f32[32,4,8,128]{3,2,1,0:T(8,128)S(1)} async-done(((f32[32,4,8,128]{3,2,1,0:T(8,128)}), f32[32,4,8,128]{3,2,1,0:T(8,128)S(1)}, u32[]{:S(2)}, u32[]{:S(2)}) %all-to-all-start) | async-done | bytes 524320 | tf_op jit(solution)/shard_map/all_to_all | solution.py:358
  32.8 1.1 %shard_map.99 = f32[128,8,128]{2,1,0:T(8,128)} custom-call(f32[1024,128]{1,0:T(8,128)S(1)} %bitcast.31, bf16[256,256]{1,0:T(8,128)(2,1)S(1)} %copy-done.1), custom_call_target="tpu_custom_call" | custom-call | flops 1000000 | bytes 1000000 | tf_op jit(solution)/shard_map/pallas_call | solution.py:385
  33.9 5.8 %all-to-all-start.1 = ((f32[32,4,8,128]{3,2,1,0:T(8,128)}), f32[32,4,8,128]{3,2,1,0:T(8,128)S(1)}, u32[]{:S(2)}, u32[]{:S(2)}) async-start(f32[32,4,8,128]{3,2,1,0:T(8,128)} %bitcast.8), calls=%async_computation.1 | async-start | bytes 1048576 | tf_op jit(solution)/shard_map/all_to_all | solution.py:392
  39.7 0.0 copy-start.2
  39.8 3.0 %collective-permute-start.5 = (f32[2,4,16,128]{3,2,1,0:T(8,128)S(1)}, f32[2,4,16,128]{3,2,1,0:T(8,128)S(1)}, u32[]{:S(2)}, u32[]{:S(2)}) collective-permute-start(f32[2,4,16,128]{3,2,1,0:T(8,128)S(1)} %dynamic-slice_bitcast_fusion.1), channel_id=1, source_target_pairs={{0,4},{1,5},{2,6},{3,7},{4,0},{5,1},{6,2},{7,3},{8,12},{9,13},{10,... | collective-permute-start | bytes 196616 | tf_op jit(solution)/shard_map/ppermute | solution.py:30
  42.8 5.3 %shard_map.96 = (f32[16,128]{1,0:T(8,128)S(1)}, f32[33,16,128]{2,1,0:T(8,128)S(1)}) custom-call(s32[816]{0:T(1024)S(1)} %get-tuple-element.6.listed_ref, f32[8,128,128]{2,1,0:T(8,128)S(1)} %bitcast.28, f32[32,8,256]{2,1,0:T(8,128)S(1)} %bitcast.33), custom_call_target="tpu_custom_call" | custom-call | flops 1000000 | bytes 1000000 | tf_op jit(solution)/shard_map/pallas_call | solution.py:363
  48.0 0.7 %collective-permute-start = (f32[16,128]{1,0:T(8,128)S(1)}, f32[16,128]{1,0:T(8,128)S(1)}, u32[]{:S(2)}, u32[]{:S(2)}) collective-permute-start(f32[16,128]{1,0:T(8,128)S(1)} %get-tuple-element.7), channel_id=1, source_target_pairs={{0,8},{8,0},{16,24},{24,16},{32,40},{40,32},{48,56},{56,48},{64,72... | collective-permute-start | bytes 24584 | tf_op jit(solution)/shard_map/ppermute | solution.py:30
  48.8 0.8 %collective-permute-done = f32[16,128]{1,0:T(8,128)S(1)} collective-permute-done((f32[16,128]{1,0:T(8,128)S(1)}, f32[16,128]{1,0:T(8,128)S(1)}, u32[]{:S(2)}, u32[]{:S(2)}) %collective-permute-start) | collective-permute-done | bytes 8224 | tf_op jit(solution)/shard_map/ppermute | solution.py:30
  49.6 2.5 %collective-permute-start.1 = (f32[16,128]{1,0:T(8,128)S(1)}, f32[16,128]{1,0:T(8,128)S(1)}, u32[]{:S(2)}, u32[]{:S(2)}) collective-permute-start(f32[16,128]{1,0:T(8,128)S(1)} %add.58), channel_id=1, source_target_pairs={{0,16},{8,24},{16,0},{24,8},{32,48},{40,56},{48,32},{56,40},{64,80... | collective-permute-start | bytes 24584 | tf_op jit(solution)/shard_map/ppermute | solution.py:30
  52.1 0.5 shard_map.97.local_ref
  52.5 1.5 %collective-permute-done.1 = f32[16,128]{1,0:T(8,128)S(1)} collective-permute-done((f32[16,128]{1,0:T(8,128)S(1)}, f32[16,128]{1,0:T(8,128)S(1)}, u32[]{:S(2)}, u32[]{:S(2)}) %collective-permute-start.1) | collective-permute-done | bytes 8224 | tf_op jit(solution)/shard_map/ppermute | solution.py:30
  54.0 2.2 %collective-permute-start.3 = (f32[16,128]{1,0:T(8,128)S(1)}, f32[16,128]{1,0:T(8,128)S(1)}, u32[]{:S(2)}, u32[]{:S(2)}) collective-permute-start(f32[16,128]{1,0:T(8,128)S(1)} %add.59), channel_id=1, source_target_pairs={{0,224},{8,232},{16,240},{24,248},{32,0},{40,8},{48,16},{56,24},{6... | collective-permute-start | bytes 24584 | tf_op jit(solution)/shard_map/ppermute | solution.py:30
  56.2 0.0 copy-start.4
  56.3 0.4 collective-permute-start.6
  56.7 0.3 collective-permute-done.3
  57.0 2.9 %collective-permute-done.2 = f32[16,128]{1,0:T(8,128)S(1)} collective-permute-done((f32[16,128]{1,0:T(8,128)S(1)}, f32[16,128]{1,0:T(8,128)S(1)}, u32[]{:S(2)}, u32[]{:S(2)}) %collective-permute-start.2) | collective-permute-done | bytes 8224 | tf_op jit(solution)/shard_map/ppermute | solution.py:30
  59.9 4.3 %shard_map.98 = f32[8,128,128]{2,1,0:T(8,128)S(1)} custom-call(s32[816]{0:T(1024)S(1)} %get-tuple-element.6.listed_ref, f32[16,128]{1,0:T(8,128)S(1)} %add_add_fusion.coef_ref, f32[16,8]{1,0:T(8,128)S(1)} %bitcast.34, f32[33,16,128]{2,1,0:T(8,128)S(1)} %get-tuple-element.8.table_ref, f32[8,128,128]{2,1,0:T(8,128)S(1)} %shard_map.97.local_ref), custom_call_target="tpu_custom_call" | custom-call | flops 1000000 | bytes 1000000 | tf_op jit(solution)/shard_map/pallas_call | solution.py:394
  64.3 0.6 bitcast_add_fusion.2
  64.9 0.9 %shard_map.100 = f32[2,4,16,8,128]{4,3,2,1,0:T(8,128)} custom-call(f32[2,4,16,8,128]{4,3,2,1,0:T(8,128)S(1)} %bitcast.32, f32[2,16,4,8,128]{4,3,2,1,0:T(8,128)S(1)} %bitcast.30), custom_call_target="tpu_custom_call" | custom-call | flops 1000000 | bytes 1000000 | tf_op jit(solution)/shard_map/pallas_call | solution.py:400
  (20 shorter events, 0.1 us)
Async XLA Ops:
  3.3 13.3 %copy-start = (f32[2,1,4,128,128]{4,3,2,1,0:T(8,128)S(1)}, f32[2,1,4,128,128]{4,3,2,1,0:T(8,128)}, u32[]{:S(2)}) copy-start(f32[2,1,4,128,128]{4,3,2,1,0:T(8,128)} %param.8) | copy-start | bytes 1572868
  3.3 29.5 %all-to-all-start = ((f32[32,4,8,128]{3,2,1,0:T(8,128)}), f32[32,4,8,128]{3,2,1,0:T(8,128)S(1)}, u32[]{:S(2)}, u32[]{:S(2)}) async-start(f32[32,4,8,128]{3,2,1,0:T(8,128)} %bitcast.6), calls=%async_computation | async-start | bytes 1048576 | tf_op jit(solution)/shard_map/all_to_all | solution.py:358
  16.7 16.1 %copy-start.1 = (bf16[256,256]{1,0:T(8,128)(2,1)S(1)}, bf16[256,256]{1,0:T(8,128)(2,1)}, u32[]{:S(2)}) copy-start(bf16[256,256]{1,0:T(8,128)(2,1)} %constant.84.clone.wide_ref) | copy-start | bytes 393220
  16.7 23.0 %collective-permute-start.4 = (f32[2,2,4,16,128]{4,3,2,1,0:T(8,128)S(1)}, f32[2,2,4,16,128]{4,3,2,1,0:T(8,128)S(1)}, u32[]{:S(2)}, u32[]{:S(2)}) collective-permute-start(f32[2,2,4,16,128]{4,3,2,1,0:T(8,128)S(1)} %dynamic-slice_bitcast_fusion), channel_id=1, source_target_pairs={{0,2},{1,3},{2,0},{3,1},{4,6},{5,7},{6,4},{7,5},{8,10},{9,11},{10,... | collective-permute-start | bytes 393224 | tf_op jit(solution)/shard_map/ppermute | solution.py:30
  33.9 31.1 %all-to-all-start.1 = ((f32[32,4,8,128]{3,2,1,0:T(8,128)}), f32[32,4,8,128]{3,2,1,0:T(8,128)S(1)}, u32[]{:S(2)}, u32[]{:S(2)}) async-start(f32[32,4,8,128]{3,2,1,0:T(8,128)} %bitcast.8), calls=%async_computation.1 | async-start | bytes 1048576 | tf_op jit(solution)/shard_map/all_to_all | solution.py:392
  39.7 3.1 %copy-start.2 = (f32[2,16,8,256]{3,2,1,0:T(8,128)S(1)}, f32[2,16,8,256]{3,2,1,0:T(8,128)}, u32[]{:S(2)}) copy-start(f32[2,16,8,256]{3,2,1,0:T(8,128)} %param.13) | copy-start | bytes 786436
  39.8 16.4 %collective-permute-start.5 = (f32[2,4,16,128]{3,2,1,0:T(8,128)S(1)}, f32[2,4,16,128]{3,2,1,0:T(8,128)S(1)}, u32[]{:S(2)}, u32[]{:S(2)}) collective-permute-start(f32[2,4,16,128]{3,2,1,0:T(8,128)S(1)} %dynamic-slice_bitcast_fusion.1), channel_id=1, source_target_pairs={{0,4},{1,5},{2,6},{3,7},{4,0},{5,1},{6,2},{7,3},{8,12},{9,13},{10,... | collective-permute-start | bytes 196616 | tf_op jit(solution)/shard_map/ppermute | solution.py:30
  42.8 9.3 %copy-start.3 = (f32[4,128,128]{2,1,0:T(8,128)S(1)}, f32[4,128,128]{2,1,0:T(8,128)}, u32[]{:S(2)}) copy-start(f32[4,128,128]{2,1,0:T(8,128)} %potential_ref.1) | copy-start | bytes 786436
  48.0 1.6 %collective-permute-start = (f32[16,128]{1,0:T(8,128)S(1)}, f32[16,128]{1,0:T(8,128)S(1)}, u32[]{:S(2)}, u32[]{:S(2)}) collective-permute-start(f32[16,128]{1,0:T(8,128)S(1)} %get-tuple-element.7), channel_id=1, source_target_pairs={{0,8},{8,0},{16,24},{24,16},{32,40},{40,32},{48,56},{56,48},{64,72... | collective-permute-start | bytes 24584 | tf_op jit(solution)/shard_map/ppermute | solution.py:30
  49.6 4.4 %collective-permute-start.1 = (f32[16,128]{1,0:T(8,128)S(1)}, f32[16,128]{1,0:T(8,128)S(1)}, u32[]{:S(2)}, u32[]{:S(2)}) collective-permute-start(f32[16,128]{1,0:T(8,128)S(1)} %add.58), channel_id=1, source_target_pairs={{0,16},{8,24},{16,0},{24,8},{32,48},{40,56},{48,32},{56,40},{64,80... | collective-permute-start | bytes 24584 | tf_op jit(solution)/shard_map/ppermute | solution.py:30
  54.0 3.0 %collective-permute-start.3 = (f32[16,128]{1,0:T(8,128)S(1)}, f32[16,128]{1,0:T(8,128)S(1)}, u32[]{:S(2)}, u32[]{:S(2)}) collective-permute-start(f32[16,128]{1,0:T(8,128)S(1)} %add.59), channel_id=1, source_target_pairs={{0,224},{8,232},{16,240},{24,248},{32,0},{40,8},{48,16},{56,24},{6... | collective-permute-start | bytes 24584 | tf_op jit(solution)/shard_map/ppermute | solution.py:30
  56.2 3.7 %collective-permute-start.2 = (f32[16,128]{1,0:T(8,128)S(1)}, f32[16,128]{1,0:T(8,128)S(1)}, u32[]{:S(2)}, u32[]{:S(2)}) collective-permute-start(f32[16,128]{1,0:T(8,128)S(1)} %add.59), channel_id=1, source_target_pairs={{0,32},{8,40},{16,48},{24,56},{32,64},{40,72},{48,80},{56,88},{64,... | collective-permute-start | bytes 24584 | tf_op jit(solution)/shard_map/ppermute | solution.py:30
  56.2 3.7 %copy-start.4 = (f32[2,8,8]{2,1,0:T(8,128)S(1)}, f32[2,8,8]{2,1,0:T(8,128)}, u32[]{:S(2)}) copy-start(f32[2,8,8]{2,1,0:T(8,128)} %param.14) | copy-start | bytes 1540
  56.3 8.0 %collective-permute-start.6 = (f32[4,16,128]{2,1,0:T(8,128)S(1)}, f32[4,16,128]{2,1,0:T(8,128)S(1)}, u32[]{:S(2)}, u32[]{:S(2)}) collective-permute-start(f32[4,16,128]{2,1,0:T(8,128)S(1)} %dynamic-slice_bitcast_fusion.2), channel_id=1, source_target_pairs={{0,1},{1,0},{2,3},{3,2},{4,5},{5,4},{6,7},{7,6},{8,9},{9,8},{10,11... | collective-permute-start | bytes 98312 | tf_op jit(solution)/shard_map/ppermute | solution.py:30

commit v3 on v2

--- a/solution.py
+++ b/solution.py
@@ -11,7 +11,6 @@
 
 spacing = 0.32
 time_step = 0.1
-highest = lax.Precision.HIGHEST
 
 SIDE = 128
 BOX = 16
@@ -19,6 +18,7 @@
 PLANES = 4
 PAD = SIDE + BOX
 GROUP = 4
+UNROLL = 8
 FIELD = 136
 COUNT = 5 * FIELD
 F32 = jnp.float32
@@ -108,8 +108,7 @@
     depth = (first_plane - centres_ref[0, atom] + (BOX // 2 + SIDE)) & (SIDE - 1)
     start_y = (centres_ref[1, atom] + (SIDE - BOX // 2)) & (SIDE - 1)
     start_z = (centres_ref[2, atom] + (SIDE - BOX // 2)) & (SIDE - 1)
-    touched = ((depth + (PLANES - 1)) & (SIDE - 1)) < BOX + PLANES - 1
-    return depth, start_y, start_z, touched
+    return depth, start_y, start_z
 
 
 def table_row(depth, plane, kind):
@@ -128,15 +127,22 @@
 def project_kernel(listed_ref, wave_ref, projectors_ref, coef_ref, table_ref, padded, sums):
     lane = lax.broadcasted_iota(jnp.int32, (8, SIDE), 1)
     row = lax.broadcasted_iota(jnp.int32, (8, SIDE), 0)
-    for index in range(2 * PLANES):
+
+    def widen(index, carry):
         padded[index, 0:SIDE, :] = wave_ref[index]
         padded[index, SIDE:PAD, :] = wave_ref[index, 0:BOX, :]
+        return carry
+
+    lax.fori_loop(0, 2 * PLANES, widen, 0)
     sums[...] = jnp.zeros_like(sums)
 
-    for index in range(2 * BOX):
+    def fill(index, carry):
         for half in range(2):
             tile = projectors_ref[index, :, half * SIDE : (half + 1) * SIDE]
             table_ref[index, half * 8 : half * 8 + 8, :] = swap_blocks(tile, lane, row)
+        return carry
+
+    lax.fori_loop(0, 2 * BOX, fill, 0, unroll=UNROLL)
     table_ref[2 * BOX] = jnp.zeros((BOX, SIDE), F32)
     inner = lane & (BOX - 1)
 
@@ -186,23 +192,29 @@
     groups = (lax.broadcasted_iota(jnp.int32, (2 * NPROJ, 2 * SIDE), 1) >> 4) == (
         lax.broadcasted_iota(jnp.int32, (2 * NPROJ, 2 * SIDE), 0)
     )
+    groups = groups.astype(F32).astype(BF16)
+    first, second = (half.astype(F32) for half in halves(coupling_ref[...]))
     mixing = lax.dot_general(
-        coupling_ref[...],
-        groups.astype(F32),
+        jnp.concatenate([first, second], axis=1).astype(BF16),
+        groups,
         (((0,), (0,)), ((), ())),
-        precision=highest,
         preferred_element_type=F32,
     )
+    both = jnp.concatenate([coef_ref[0:8, :], coef_ref[8:16, :]], axis=1)
+    first, second = (half.astype(F32) for half in halves(both))
     scaled[...] = lax.dot_general(
-        jnp.concatenate([coef_ref[0:8, :], coef_ref[8:16, :]], axis=1),
-        mixing,
+        jnp.concatenate([first, first, second], axis=0).astype(BF16),
+        jnp.concatenate([mixing[0:8], mixing[8:16], mixing[0:8]], axis=0).astype(BF16),
         (((0,), (0,)), ((), ())),
-        precision=highest,
         preferred_element_type=F32,
     )
-    for index in range(2 * PLANES):
+
+    def widen(index, carry):
         padded[index, 0:SIDE, :] = local_ref[index]
         padded[index, SIDE:PAD, :] = jnp.zeros((BOX, SIDE), F32)
+        return carry
+
+    lax.fori_loop(0, 2 * PLANES, widen, 0)
 
     def group_step(step, carry):
         for offset in range(GROUP):
@@ -228,9 +240,13 @@
         return carry
 
     lax.fori_loop(0, group_count(listed_ref), group_step, 0)
-    for index in range(2 * PLANES):
+
+    def narrow(index, carry):
         out_ref[index, 0:BOX, :] = padded[index, 0:BOX, :] + padded[index, SIDE:PAD, :]
         out_ref[index, BOX:SIDE, :] = padded[index, BOX:SIDE, :]
+        return carry
+
+    lax.fori_loop(0, 2 * PLANES, narrow, 0)
 
 
 def local_kernel(wave_ref, potential_ref, wide_ref, out_ref):
@@ -252,19 +268,24 @@
         copy.wait()
 
 
-def list_atoms(first_plane, centres_ref, species_ref, listed_ref):
+def list_part(first_plane, centres_ref, listed_ref, start, stop, count):
+    top = first_plane + (BOX // 2 + SIDE + PLANES - 1)
+
     def list_step(atom, count):
-        touched = atom_place(first_plane, centres_ref, atom)[3]
+        reach = (top - centres_ref[0, atom]) & (SIDE - 1)
         listed_ref[count] = atom
-        return count + touched.astype(jnp.int32)
-
-    count = lax.fori_loop(0, SIDE, list_step, 0, unroll=8)
+        return count + jnp.where(reach < BOX + PLANES - 1, 1, 0)
+
+    return lax.fori_loop(start, stop, list_step, count, unroll=8)
+
+
+def list_details(first_plane, centres_ref, species_ref, listed_ref, count):
     listed_ref[COUNT] = count
 
     def detail_step(index, carry):
         atom = listed_ref[index]
-        depth, start_y, start_z, _ = atom_place(first_plane, centres_ref, atom)
-        for field, value in enumerate((depth, start_y, start_z, species_ref[atom])):
+        place = atom_place(first_plane, centres_ref, atom)
+        for field, value in enumerate((*place, species_ref[atom])):
             listed_ref[(field + 1) * FIELD + index] = value
         return carry
 
@@ -304,21 +325,27 @@
     listing = pltpu.make_async_copy(listed, listed_out_ref, list_sems.at[2])
     for copy in tables + arriving:
         copy.start()
-    for first, second in zip(arriving, leaving):
-        first.wait()
-        second.start()
     for copy in tables:
         copy.wait()
-    list_atoms(first_ref[0], centres, species, listed)
+    count = jnp.int32(0)
+    for slot in range(2 * PLANES):
+        if slot % 2 == 0:
+            share = SIDE // PLANES
+            count = list_part(first_ref[0], centres, listed, slot // 2 * share, (slot // 2 + 1) * share, count)
+        arriving[slot].wait()
+        leaving[slot].start()
+    list_details(first_ref[0], centres, species, listed, count)
     listing.start()
     for copy in leaving:
         copy.wait()
     listing.wait()
 
 
-def final_kernel(local_ref, depth_ref, out_ref, held, sems):
+def final_kernel(local_ref, depth_ref, mine_ref, first_ref, second_ref, third_ref, out_ref, density_ref, held, sums, sems):
     half_step = 0.5 * time_step
-    copies = []
+    sums[...] = (mine_ref[...] + first_ref[...]) + (second_ref[...] + third_ref[...])
+    copies = [pltpu.make_async_copy(sums, density_ref, sems.at[2 * PLANES])]
+    copies[-1].start()
     for plane in range(PLANES):
         for part, sign in ((0, half_step), (1, -half_step)):
             held[part, plane] = sign * (local_ref[1 - part, plane] + depth_ref[1 - part, :, plane])
@@ -375,12 +402,20 @@
     local = call(local_kernel, shape(2 * PLANES, SIDE, SIDE), [vmem] * 3)(planes, potential, wide)
 
     place = lax.axis_index("orb")
-    for bit in (2, 4, 1):
-        mine = (place // bit) % 2
-        kept = lax.dynamic_index_in_dim(terms, mine, 0, keepdims=False)
-        given = lax.dynamic_index_in_dim(terms, 1 - mine, 0, keepdims=False)
-        terms = kept + permuted(given, "orb", lambda source: source ^ bit)
-    density = terms
+    middle, high_bit, low_bit = place // 2 % 2, place // 4, place % 2
+    kept = lax.dynamic_index_in_dim(terms, middle, 0, keepdims=False)
+    given = lax.dynamic_index_in_dim(terms, 1 - middle, 0, keepdims=False)
+    terms = kept + permuted(given, "orb", lambda source: source ^ 2)
+
+    def share_of(high, low):
+        return lax.dynamic_slice(terms, (high, low, 0, 0, 0), (1, 1, PLANES, 16, SIDE))[0, 0]
+
+    shares = [
+        share_of(high_bit, low_bit),
+        permuted(share_of(1 - high_bit, low_bit), "orb", lambda source: source ^ 4),
+        permuted(share_of(high_bit, 1 - low_bit), "orb", lambda source: source ^ 1),
+        permuted(share_of(1 - high_bit, 1 - low_bit), "orb", lambda source: source ^ 5),
+    ]
 
     depth = call(
         depth_kernel,
@@ -397,14 +432,20 @@
         [smem, vmem, vmem, vmem, vmem],
         [pltpu.VMEM((2 * PLANES, PAD, SIDE), F32), pltpu.VMEM((2 * SIDE, 2 * SIDE), F32)],
     )(listed, total_coef, coupling.reshape(2 * NPROJ, NPROJ), table, local)
-    update = call(
+    update, density = call(
         final_kernel,
-        shape(2, PLANES, blocks, 8, SIDE),
-        [vmem] * 2,
-        [pltpu.VMEM((2, PLANES, blocks, 8, SIDE), F32), pltpu.SemaphoreType.DMA((2 * PLANES,))],
-        outs=outside,
+        (shape(2, PLANES, blocks, 8, SIDE), shape(PLANES, 16, SIDE)),
+        [vmem] * 6,
+        [
+            pltpu.VMEM((2, PLANES, blocks, 8, SIDE), F32),
+            pltpu.VMEM((PLANES, 16, SIDE), F32),
+            pltpu.SemaphoreType.DMA((2 * PLANES + 1,)),
+        ],
+        outs=(outside, outside),
     )(
-        total.reshape(2, PLANES, blocks, 8, SIDE), returned.reshape(2, blocks, PLANES, 8, SIDE)
+        total.reshape(2, PLANES, blocks, 8, SIDE),
+        returned.reshape(2, blocks, PLANES, 8, SIDE),
+        *shares,
     )
     return (update.reshape(wave.shape), density)
 

time: 66.9 us -> 64.9 us (0.970)
  the two profiles are of different devices: /device:TPU:1 before, /device:TPU:4 now
where the time goes in v3:
time: 64.9 us; the launch traced here: 64.6 us
  blocking collectives  29.2 us (45%)
  starting transfers between devices  15.9 us (24%)
  Pallas kernels  10.5 us (16%)
  waiting for transfers between devices  7.57 us (12%)
  between operations  1.46 us (2%)
    all_to_all x1, blocking collectives, whole_step(): columns = lax.all_to_all(sent, 'grid', 0, 0, tiled=True)  29.2 us
    ppermute x8, starting transfers between devices, permuted(): lax.ppermute(value, axis, [(source, target(source) % count) for source in...  10.7 us
    ppermute x8, waiting for transfers between devices, permuted(): lax.ppermute(value, axis, [(source, target(source) % count) for source in...  7.56 us
    all_to_all x1, starting transfers between devices, whole_step(): lax.all_to_all(depth.reshape(2 * blocks, PLANES, 8, SIDE), 'grid', 0, 0,...  5.13 us
    pallas_call x1, Pallas kernels, whole_step(): call(spread_kernel, shape(2 * PLANES, SIDE, SIDE), [smem, vmem, vmem, vme...  3.21 us
    pallas_call x1, Pallas kernels, whole_step(): call(project_kernel, (shape(2 * NPROJ, SIDE), shape(2 * BOX + 1, BOX, SID...  2.49 us
    pallas_call x1, Pallas kernels, whole_step(): call(pack_kernel, (shape(2, blocks, PLANES, 8, SIDE), jax.ShapeDtypeStruc...  2.31 us
  transfers between devices with their start and end apart: 9, of which 3 were waited for; matrix products, arithmetic and copies ran while one was open for 0% of the time, Pallas kernels for 10%

profile of v3, /device:TPU:4, one launch (start us, length us, event | category | flops | bytes accessed | tf_op | source)
XLA Modules:
  0.0 64.6 jit_solution(4591844661734669187)
XLA Ops:
  0.6 2.3 %shard_map.95 = (f32[2,16,4,8,128]{4,3,2,1,0:T(8,128)S(1)}, s32[816]{0:T(1024)S(1)}) custom-call(s32[1]{0:T(128)} %bitcast.first_ref, f32[2,4,16,8,128]{4,3,2,1,0:T(8,128)} %bitcast.26, s32[3,128]{1,0:T(4,128)} %centres_ref.1, s32[128]{0:T(128)} %species_ref.1), custom_call_target="tpu_custom_call" | custom-call | flops 1000000 | bytes 1000000 | tf_op jit(solution)/shard_map/pallas_call | solution.py:369
  3.0 0.0 copy-start.1
  3.0 29.2 %all_to_all.10 = f32[32,4,8,128]{3,2,1,0:T(8,128)S(1)} all-to-all(f32[32,4,8,128]{3,2,1,0:T(8,128)S(1)} %bitcast.33), channel_id=1, replica_groups=mesh['grid'=32,'orb'=8] {'grid'}, dimensions={0} | all-to-all | bytes 1048576 | tf_op jit(solution)/shard_map/all_to_all | solution.py:385
  32.2 1.1 %shard_map.99 = f32[128,8,128]{2,1,0:T(8,128)} custom-call(f32[1024,128]{1,0:T(8,128)S(1)} %bitcast.31, bf16[256,256]{1,0:T(8,128)(2,1)S(1)} %copy-done.1), custom_call_target="tpu_custom_call" | custom-call | flops 1000000 | bytes 1000000 | tf_op jit(solution)/shard_map/pallas_call | solution.py:420
  33.2 0.0 copy-start
  33.2 5.1 %all-to-all-start.1 = ((f32[32,4,8,128]{3,2,1,0:T(8,128)}), f32[32,4,8,128]{3,2,1,0:T(8,128)S(1)}, u32[]{:S(2)}, u32[]{:S(2)}) async-start(f32[32,4,8,128]{3,2,1,0:T(8,128)} %bitcast.8), calls=%async_computation.1 | async-start | bytes 1048576 | tf_op jit(solution)/shard_map/all_to_all | solution.py:427
  39.1 0.0 copy-start.2
  39.1 1.7 %collective-permute-start.4 = (f32[2,2,4,16,128]{4,3,2,1,0:T(8,128)S(1)}, f32[2,2,4,16,128]{4,3,2,1,0:T(8,128)S(1)}, u32[]{:S(2)}, u32[]{:S(2)}) collective-permute-start(f32[2,2,4,16,128]{4,3,2,1,0:T(8,128)S(1)} %dynamic-slice_bitcast_fusion), channel_id=1, source_target_pairs={{0,2},{1,3},{2,0},{3,1},{4,6},{5,7},{6,4},{7,5},{8,10},{9,11},{10,... | collective-permute-start | bytes 393224 | tf_op jit(solution)/shard_map/ppermute | solution.py:30
  40.8 2.5 %shard_map.96 = (f32[16,128]{1,0:T(8,128)S(1)}, f32[33,16,128]{2,1,0:T(8,128)S(1)}) custom-call(s32[816]{0:T(1024)S(1)} %get-tuple-element.8.listed_ref, f32[8,128,128]{2,1,0:T(8,128)S(1)} %bitcast.28, f32[32,8,256]{2,1,0:T(8,128)S(1)} %bitcast.34), custom_call_target="tpu_custom_call" | custom-call | flops 1000000 | bytes 1000000 | tf_op jit(solution)/shard_map/pallas_call | solution.py:390
  43.3 0.0 collective-permute-start
  43.4 1.2 %collective-permute-done = f32[16,128]{1,0:T(8,128)S(1)} collective-permute-done((f32[16,128]{1,0:T(8,128)S(1)}, f32[16,128]{1,0:T(8,128)S(1)}, u32[]{:S(2)}, u32[]{:S(2)}) %collective-permute-start) | collective-permute-done | bytes 8224 | tf_op jit(solution)/shard_map/ppermute | solution.py:30
  44.5 0.8 %collective-permute-start.1 = (f32[16,128]{1,0:T(8,128)S(1)}, f32[16,128]{1,0:T(8,128)S(1)}, u32[]{:S(2)}, u32[]{:S(2)}) collective-permute-start(f32[16,128]{1,0:T(8,128)S(1)} %add.50), channel_id=1, source_target_pairs={{0,16},{8,24},{16,0},{24,8},{32,48},{40,56},{48,32},{56,40},{64,80... | collective-permute-start | bytes 24584 | tf_op jit(solution)/shard_map/ppermute | solution.py:30
  45.3 0.5 shard_map.97.local_ref
  45.7 3.9 %collective-permute-done.1 = f32[16,128]{1,0:T(8,128)S(1)} collective-permute-done((f32[16,128]{1,0:T(8,128)S(1)}, f32[16,128]{1,0:T(8,128)S(1)}, u32[]{:S(2)}, u32[]{:S(2)}) %collective-permute-start.1) | collective-permute-done | bytes 8224 | tf_op jit(solution)/shard_map/ppermute | solution.py:30
  49.7 3.2 %collective-permute-start.3 = (f32[16,128]{1,0:T(8,128)S(1)}, f32[16,128]{1,0:T(8,128)S(1)}, u32[]{:S(2)}, u32[]{:S(2)}) collective-permute-start(f32[16,128]{1,0:T(8,128)S(1)} %add.51), channel_id=1, source_target_pairs={{0,224},{8,232},{16,240},{24,248},{32,0},{40,8},{48,16},{56,24},{6... | collective-permute-start | bytes 24584 | tf_op jit(solution)/shard_map/ppermute | solution.py:30
  52.9 0.0 copy-start.4
  53.0 3.3 %collective-permute-start.5 = (f32[4,16,128]{2,1,0:T(8,128)S(1)}, f32[4,16,128]{2,1,0:T(8,128)S(1)}, u32[]{:S(2)}, u32[]{:S(2)}) collective-permute-start(f32[4,16,128]{2,1,0:T(8,128)S(1)} %get-tuple-element.18), channel_id=1, source_target_pairs={{0,4},{1,5},{2,6},{3,7},{4,0},{5,1},{6,2},{7,3},{8,12},{9,13},{10,... | collective-permute-start | bytes 98312 | tf_op jit(solution)/shard_map/ppermute | solution.py:30
  56.2 1.2 %collective-permute-start.6 = (f32[4,16,128]{2,1,0:T(8,128)S(1)}, f32[4,16,128]{2,1,0:T(8,128)S(1)}, u32[]{:S(2)}, u32[]{:S(2)}) collective-permute-start(f32[4,16,128]{2,1,0:T(8,128)S(1)} %get-tuple-element.17), channel_id=1, source_target_pairs={{0,1},{1,0},{2,3},{3,2},{4,5},{5,4},{6,7},{7,6},{8,9},{9,8},{10,11... | collective-permute-start | bytes 98312 | tf_op jit(solution)/shard_map/ppermute | solution.py:30
  57.4 0.6 collective-permute-start.7
  58.0 0.0 collective-permute-done.3
  58.0 0.0 collective-permute-done.2
  58.1 3.2 %shard_map.98 = f32[8,128,128]{2,1,0:T(8,128)S(1)} custom-call(s32[816]{0:T(1024)S(1)} %get-tuple-element.8.listed_ref, f32[16,128]{1,0:T(8,128)S(1)} %add_add_fusion.coef_ref, f32[16,8]{1,0:T(8,128)S(1)} %bitcast.35, f32[33,16,128]{2,1,0:T(8,128)S(1)} %get-tuple-element.10.table_ref, f32[8,128,128]{2,1,0:T(8,128)S(1)} %shard_map.97.local_ref), custom_call_target="tpu_custom_call" | custom-call | flops 1000000 | bytes 1000000 | tf_op jit(solution)/shard_map/pallas_call | solution.py:429
  61.3 2.5 %collective-permute-done.7.third_ref = f32[4,16,128]{2,1,0:T(8,128)S(1)} collective-permute-done((f32[4,16,128]{2,1,0:T(8,128)S(1)}, f32[4,16,128]{2,1,0:T(8,128)S(1)}, u32[]{:S(2)}, u32[]{:S(2)}) %collective-permute-start.7) | collective-permute-done | bytes 32800 | tf_op jit(solution)/shard_map/ppermute | solution.py:30
  63.7 0.9 %shard_map.101 = (f32[2,4,16,8,128]{4,3,2,1,0:T(8,128)}, f32[4,16,128]{2,1,0:T(8,128)}) custom-call(f32[2,4,16,8,128]{4,3,2,1,0:T(8,128)S(1)} %bitcast.32, f32[2,16,4,8,128]{4,3,2,1,0:T(8,128)S(1)} %bitcast.30, f32[4,16,128]{2,1,0:T(8,128)S(1)} %get-tuple-element.19.mine_ref, f32[4,16,128]{2,1,0:T(8,128)S(1)} %collective-permute-done.5.first_ref, ...), custom_call_target="tpu_custom_call" | custom-call | flops 1000000 | bytes 1000000 | tf_op jit(solution)/shard_map/pallas_call | solution.py:435
  (18 shorter events, 0.1 us)
Async XLA Ops:
  3.0 29.2 %copy-start.1 = (bf16[256,256]{1,0:T(8,128)(2,1)S(1)}, bf16[256,256]{1,0:T(8,128)(2,1)}, u32[]{:S(2)}) copy-start(bf16[256,256]{1,0:T(8,128)(2,1)} %constant.61.clone.wide_ref) | copy-start | bytes 393220
  33.2 5.8 %copy-start = (f32[2,1,4,128,128]{4,3,2,1,0:T(8,128)S(1)}, f32[2,1,4,128,128]{4,3,2,1,0:T(8,128)}, u32[]{:S(2)}) copy-start(f32[2,1,4,128,128]{4,3,2,1,0:T(8,128)} %param.8) | copy-start | bytes 1572868
  33.2 30.5 %all-to-all-start.1 = ((f32[32,4,8,128]{3,2,1,0:T(8,128)}), f32[32,4,8,128]{3,2,1,0:T(8,128)S(1)}, u32[]{:S(2)}, u32[]{:S(2)}) async-start(f32[32,4,8,128]{3,2,1,0:T(8,128)} %bitcast.8), calls=%async_computation.1 | async-start | bytes 1048576 | tf_op jit(solution)/shard_map/all_to_all | solution.py:427
  39.1 1.7 %copy-start.2 = (f32[2,16,8,256]{3,2,1,0:T(8,128)S(1)}, f32[2,16,8,256]{3,2,1,0:T(8,128)}, u32[]{:S(2)}) copy-start(f32[2,16,8,256]{3,2,1,0:T(8,128)} %param.13) | copy-start | bytes 786436
  39.1 13.7 %collective-permute-start.4 = (f32[2,2,4,16,128]{4,3,2,1,0:T(8,128)S(1)}, f32[2,2,4,16,128]{4,3,2,1,0:T(8,128)S(1)}, u32[]{:S(2)}, u32[]{:S(2)}) collective-permute-start(f32[2,2,4,16,128]{4,3,2,1,0:T(8,128)S(1)} %dynamic-slice_bitcast_fusion), channel_id=1, source_target_pairs={{0,2},{1,3},{2,0},{3,1},{4,6},{5,7},{6,4},{7,5},{8,10},{9,11},{10,... | collective-permute-start | bytes 393224 | tf_op jit(solution)/shard_map/ppermute | solution.py:30
  40.8 4.5 %copy-start.3 = (f32[4,128,128]{2,1,0:T(8,128)S(1)}, f32[4,128,128]{2,1,0:T(8,128)}, u32[]{:S(2)}) copy-start(f32[4,128,128]{2,1,0:T(8,128)} %potential_ref.1) | copy-start | bytes 786436
  43.3 1.2 %collective-permute-start = (f32[16,128]{1,0:T(8,128)S(1)}, f32[16,128]{1,0:T(8,128)S(1)}, u32[]{:S(2)}, u32[]{:S(2)}) collective-permute-start(f32[16,128]{1,0:T(8,128)S(1)} %get-tuple-element.9), channel_id=1, source_target_pairs={{0,8},{8,0},{16,24},{24,16},{32,40},{40,32},{48,56},{56,48},{64,72... | collective-permute-start | bytes 24584 | tf_op jit(solution)/shard_map/ppermute | solution.py:30
  44.5 5.2 %collective-permute-start.1 = (f32[16,128]{1,0:T(8,128)S(1)}, f32[16,128]{1,0:T(8,128)S(1)}, u32[]{:S(2)}, u32[]{:S(2)}) collective-permute-start(f32[16,128]{1,0:T(8,128)S(1)} %add.50), channel_id=1, source_target_pairs={{0,16},{8,24},{16,0},{24,8},{32,48},{40,56},{48,32},{56,40},{64,80... | collective-permute-start | bytes 24584 | tf_op jit(solution)/shard_map/ppermute | solution.py:30
  49.7 8.3 %collective-permute-start.3 = (f32[16,128]{1,0:T(8,128)S(1)}, f32[16,128]{1,0:T(8,128)S(1)}, u32[]{:S(2)}, u32[]{:S(2)}) collective-permute-start(f32[16,128]{1,0:T(8,128)S(1)} %add.51), channel_id=1, source_target_pairs={{0,224},{8,232},{16,240},{24,248},{32,0},{40,8},{48,16},{56,24},{6... | collective-permute-start | bytes 24584 | tf_op jit(solution)/shard_map/ppermute | solution.py:30
  52.9 5.2 %collective-permute-start.2 = (f32[16,128]{1,0:T(8,128)S(1)}, f32[16,128]{1,0:T(8,128)S(1)}, u32[]{:S(2)}, u32[]{:S(2)}) collective-permute-start(f32[16,128]{1,0:T(8,128)S(1)} %add.51), channel_id=1, source_target_pairs={{0,32},{8,40},{16,48},{24,56},{32,64},{40,72},{48,80},{56,88},{64,... | collective-permute-start | bytes 24584 | tf_op jit(solution)/shard_map/ppermute | solution.py:30
  52.9 5.1 %copy-start.4 = (f32[2,8,8]{2,1,0:T(8,128)S(1)}, f32[2,8,8]{2,1,0:T(8,128)}, u32[]{:S(2)}) copy-start(f32[2,8,8]{2,1,0:T(8,128)} %param.14) | copy-start | bytes 1540
  53.0 8.3 %collective-permute-start.5 = (f32[4,16,128]{2,1,0:T(8,128)S(1)}, f32[4,16,128]{2,1,0:T(8,128)S(1)}, u32[]{:S(2)}, u32[]{:S(2)}) collective-permute-start(f32[4,16,128]{2,1,0:T(8,128)S(1)} %get-tuple-element.18), channel_id=1, source_target_pairs={{0,4},{1,5},{2,6},{3,7},{4,0},{5,1},{6,2},{7,3},{8,12},{9,13},{10,... | collective-permute-start | bytes 98312 | tf_op jit(solution)/shard_map/ppermute | solution.py:30
  56.2 5.0 %collective-permute-start.6 = (f32[4,16,128]{2,1,0:T(8,128)S(1)}, f32[4,16,128]{2,1,0:T(8,128)S(1)}, u32[]{:S(2)}, u32[]{:S(2)}) collective-permute-start(f32[4,16,128]{2,1,0:T(8,128)S(1)} %get-tuple-element.17), channel_id=1, source_target_pairs={{0,1},{1,0},{2,3},{3,2},{4,5},{5,4},{6,7},{7,6},{8,9},{9,8},{10,11... | collective-permute-start | bytes 98312 | tf_op jit(solution)/shard_map/ppermute | solution.py:30
  57.4 6.3 %collective-permute-start.7 = (f32[4,16,128]{2,1,0:T(8,128)S(1)}, f32[4,16,128]{2,1,0:T(8,128)S(1)}, u32[]{:S(2)}, u32[]{:S(2)}) collective-permute-start(f32[4,16,128]{2,1,0:T(8,128)S(1)} %get-tuple-element.16), channel_id=1, source_target_pairs={{0,5},{1,4},{2,7},{3,6},{4,1},{5,0},{6,3},{7,2},{8,13},{9,12},{10,... | collective-permute-start | bytes 98312 | tf_op jit(solution)/shard_map/ppermute | solution.py:30

commit v4 on v3

--- a/solution.py
+++ b/solution.py
@@ -124,7 +124,27 @@
     return (listed_ref[COUNT] + (GROUP - 1)) // GROUP
 
 
-def project_kernel(listed_ref, wave_ref, projectors_ref, coef_ref, table_ref, padded, sums):
+def project_kernel(
+    first_ref,
+    centres_ref,
+    species_ref,
+    wave_ref,
+    projectors_ref,
+    coef_ref,
+    table_ref,
+    listed_ref,
+    padded,
+    sums,
+    centres,
+    species,
+    sems,
+):
+    arriving = [
+        pltpu.make_async_copy(centres_ref, centres, sems.at[0]),
+        pltpu.make_async_copy(species_ref, species, sems.at[1]),
+    ]
+    for copy in arriving:
+        copy.start()
     lane = lax.broadcasted_iota(jnp.int32, (8, SIDE), 1)
     row = lax.broadcasted_iota(jnp.int32, (8, SIDE), 0)
 
@@ -144,6 +164,10 @@
 
     lax.fori_loop(0, 2 * BOX, fill, 0, unroll=UNROLL)
     table_ref[2 * BOX] = jnp.zeros((BOX, SIDE), F32)
+    for copy in arriving:
+        copy.wait()
+    count = list_part(first_ref[0], centres, listed_ref, 0, SIDE, jnp.int32(0))
+    list_details(first_ref[0], centres, species, listed_ref, count)
     inner = lane & (BOX - 1)
 
     def group_step(step, carry):
@@ -295,21 +319,7 @@
             listed_ref[field * FIELD + count + extra] = jnp.int32(value)
 
 
-def pack_kernel(
-    first_ref,
-    wave_ref,
-    centres_ref,
-    species_ref,
-    out_ref,
-    listed_out_ref,
-    held,
-    centres,
-    species,
-    listed,
-    in_sems,
-    out_sems,
-    list_sems,
-):
+def pack_kernel(wave_ref, out_ref, held, in_sems, out_sems):
     places = [(part, plane) for part in range(2) for plane in range(PLANES)]
     arriving = [
         pltpu.make_async_copy(wave_ref.at[place], held.at[place], in_sems.at[slot]) for slot, place in enumerate(places)
@@ -318,27 +328,13 @@
         pltpu.make_async_copy(held.at[part, plane], out_ref.at[part, :, plane], out_sems.at[slot])
         for slot, (part, plane) in enumerate(places)
     ]
-    tables = [
-        pltpu.make_async_copy(centres_ref, centres, list_sems.at[0]),
-        pltpu.make_async_copy(species_ref, species, list_sems.at[1]),
-    ]
-    listing = pltpu.make_async_copy(listed, listed_out_ref, list_sems.at[2])
-    for copy in tables + arriving:
+    for copy in arriving:
         copy.start()
-    for copy in tables:
-        copy.wait()
-    count = jnp.int32(0)
-    for slot in range(2 * PLANES):
-        if slot % 2 == 0:
-            share = SIDE // PLANES
-            count = list_part(first_ref[0], centres, listed, slot // 2 * share, (slot // 2 + 1) * share, count)
-        arriving[slot].wait()
-        leaving[slot].start()
-    list_details(first_ref[0], centres, species, listed, count)
-    listing.start()
+    for first, second in zip(arriving, leaving):
+        first.wait()
+        second.start()
     for copy in leaving:
         copy.wait()
-    listing.wait()
 
 
 def final_kernel(local_ref, depth_ref, mine_ref, first_ref, second_ref, third_ref, out_ref, density_ref, held, sums, sems):
@@ -357,6 +353,10 @@
         copy.wait()
 
 
+def in_place(value):
+    return pltpu.with_memory_space_constraint(value, pltpu.HBM)
+
+
 def whole_step(wave, potential, occupations, centres, species, projectors, coupling):
     vmem, smem, outside = whole(), whole(pltpu.SMEM), whole(pl.ANY)
     wide = kinetic_halves(SIDE)
@@ -366,33 +366,39 @@
     planes = wave.reshape(2 * PLANES, SIDE, SIDE)
     table_in = projectors.reshape(2 * BOX, NPROJ, BOX * BOX)
 
-    sent, listed = call(
+    sent = call(
         pack_kernel,
-        (shape(2, blocks, PLANES, 8, SIDE), jax.ShapeDtypeStruct((COUNT + FIELD,), jnp.int32)),
-        [smem] + [whole(pltpu.HBM)] * 3,
+        shape(2, blocks, PLANES, 8, SIDE),
+        [whole(pltpu.HBM)],
         [
             pltpu.VMEM((2, PLANES, blocks, 8, SIDE), F32),
+            pltpu.SemaphoreType.DMA((2 * PLANES,)),
+            pltpu.SemaphoreType.DMA((2 * PLANES,)),
+        ],
+        outs=outside,
+    )(in_place(tiles)).reshape(2 * blocks, PLANES, 8, SIDE)
+    columns = lax.all_to_all(sent, "grid", 0, 0, tiled=True)
+
+    terms = call(density_kernel, shape(2, 2, 2, PLANES, 16, SIDE), [smem, vmem])(
+        occupations, wave.reshape(2, PLANES, SIDE, SIDE)
+    )
+    coef, table, listed = call(
+        project_kernel,
+        (
+            shape(2 * NPROJ, SIDE),
+            shape(2 * BOX + 1, BOX, SIDE),
+            jax.ShapeDtypeStruct((COUNT + FIELD,), jnp.int32),
+        ),
+        [smem, whole(pltpu.HBM), whole(pltpu.HBM), vmem, vmem],
+        [
+            pltpu.VMEM((2 * PLANES, PAD, SIDE), F32),
+            pltpu.VMEM((2, SIDE + 8, SIDE), F32),
             pltpu.SMEM((3, SIDE), jnp.int32),
             pltpu.SMEM((SIDE,), jnp.int32),
-            pltpu.SMEM((COUNT + FIELD,), jnp.int32),
-            pltpu.SemaphoreType.DMA((2 * PLANES,)),
-            pltpu.SemaphoreType.DMA((2 * PLANES,)),
-            pltpu.SemaphoreType.DMA((3,)),
+            pltpu.SemaphoreType.DMA((2,)),
         ],
-        outs=(outside, outside),
-    )(first_plane, *(pltpu.with_memory_space_constraint(value, pltpu.HBM) for value in (tiles, centres, species)))
-    sent = sent.reshape(2 * blocks, PLANES, 8, SIDE)
-    columns = lax.all_to_all(sent, "grid", 0, 0, tiled=True)
-
-    terms = call(density_kernel, shape(2, 2, 2, PLANES, 16, SIDE), [smem, vmem])(
-        occupations, wave.reshape(2, PLANES, SIDE, SIDE)
-    )
-    coef, table = call(
-        project_kernel,
-        (shape(2 * NPROJ, SIDE), shape(2 * BOX + 1, BOX, SIDE)),
-        [smem, vmem, vmem],
-        [pltpu.VMEM((2 * PLANES, PAD, SIDE), F32), pltpu.VMEM((2, SIDE + 8, SIDE), F32)],
-    )(listed, planes, table_in)
+        outs=(vmem, vmem, smem),
+    )(first_plane, in_place(centres), in_place(species), planes, table_in)
     coef = coef + permuted(coef, "grid", lambda place: place ^ 1)
     coef = coef + permuted(coef, "grid", lambda place: place ^ 2)
     above = permuted(coef, "grid", lambda place: place + 4)

time: 64.9 us -> 64 us (0.986)
  the two profiles are of different devices: /device:TPU:4 before, /device:TPU:100 now
where the time goes in v4:
time: 64 us; the launch traced here: 63.6 us
  blocking collectives  24.7 us (39%)
  starting transfers between devices  18.7 us (29%)
  Pallas kernels  12.1 us (19%)
  waiting for transfers between devices  5.9 us (9%)
  between operations  1.48 us (2%)
  local copies, waits for them, and re-layouts  0.75 us (1%)
    all_to_all x1, blocking collectives, whole_step(): columns = lax.all_to_all(sent, 'grid', 0, 0, tiled=True)  24.7 us
    ppermute x8, starting transfers between devices, permuted(): lax.ppermute(value, axis, [(source, target(source) % count) for source in...  10.4 us
    all_to_all x1, starting transfers between devices, whole_step(): lax.all_to_all(depth.reshape(2 * blocks, PLANES, 8, SIDE), 'grid', 0, 0,...  8.29 us
    ppermute x8, waiting for transfers between devices, permuted(): lax.ppermute(value, axis, [(source, target(source) % count) for source in...  5.89 us
    pallas_call x1, Pallas kernels, whole_step(): call(spread_kernel, shape(2 * PLANES, SIDE, SIDE), [smem, vmem, vmem, vme...  4.78 us
    pallas_call x1, Pallas kernels, whole_step(): call(project_kernel, (shape(2 * NPROJ, SIDE), shape(2 * BOX + 1, BOX, SID...  3.68 us
  transfers between devices with their start and end apart: 9, of which 2 were waited for; matrix products, arithmetic and copies ran while one was open for 0% of the time, Pallas kernels for 14%

profile of v4, /device:TPU:100, one launch (start us, length us, event | category | flops | bytes accessed | tf_op | source)
XLA Modules:
  0.0 63.6 jit_solution(16754875141926469746)
XLA Ops:
  0.6 1.2 %shard_map.98 = f32[2,16,4,8,128]{4,3,2,1,0:T(8,128)S(1)} custom-call(f32[2,4,16,8,128]{4,3,2,1,0:T(8,128)} %bitcast.26), custom_call_target="tpu_custom_call" | custom-call | flops 1000000 | bytes 1000000 | tf_op jit(solution)/shard_map/pallas_call | solution.py:369
  1.9 0.0 copy-start.1
  1.9 24.7 %all_to_all.10 = f32[32,4,8,128]{3,2,1,0:T(8,128)S(1)} all-to-all(f32[32,4,8,128]{3,2,1,0:T(8,128)S(1)} %bitcast.32), channel_id=1, replica_groups=mesh['grid'=32,'orb'=8] {'grid'}, dimensions={0} | all-to-all | bytes 1048576 | tf_op jit(solution)/shard_map/all_to_all | solution.py:380
  26.5 1.1 %shard_map.99 = f32[128,8,128]{2,1,0:T(8,128)} custom-call(f32[1024,128]{1,0:T(8,128)S(1)} %bitcast.31, bf16[256,256]{1,0:T(8,128)(2,1)S(1)} %copy-done.1), custom_call_target="tpu_custom_call" | custom-call | flops 1000000 | bytes 1000000 | tf_op jit(solution)/shard_map/pallas_call | solution.py:426
  27.6 0.0 copy-start
  27.6 8.3 %all-to-all-start.1 = ((f32[32,4,8,128]{3,2,1,0:T(8,128)}), f32[32,4,8,128]{3,2,1,0:T(8,128)S(1)}, u32[]{:S(2)}, u32[]{:S(2)}) async-start(f32[32,4,8,128]{3,2,1,0:T(8,128)} %bitcast.8), calls=%async_computation.1 | async-start | bytes 1048576 | tf_op jit(solution)/shard_map/all_to_all | solution.py:433
  36.7 0.0 copy-start.2
  36.7 1.7 %collective-permute-start.4 = (f32[2,2,4,16,128]{4,3,2,1,0:T(8,128)S(1)}, f32[2,2,4,16,128]{4,3,2,1,0:T(8,128)S(1)}, u32[]{:S(2)}, u32[]{:S(2)}) collective-permute-start(f32[2,2,4,16,128]{4,3,2,1,0:T(8,128)S(1)} %dynamic-slice_bitcast_fusion), channel_id=1, source_target_pairs={{0,2},{1,3},{2,0},{3,1},{4,6},{5,7},{6,4},{7,5},{8,10},{9,11},{10,... | collective-permute-start | bytes 393224 | tf_op jit(solution)/shard_map/ppermute | solution.py:30
  38.4 3.7 %shard_map.95 = (f32[16,128]{1,0:T(8,128)S(1)}, f32[33,16,128]{2,1,0:T(8,128)S(1)}, s32[816]{0:T(1024)S(1)}) custom-call(s32[1]{0:T(128)} %bitcast.first_ref, s32[3,128]{1,0:T(4,128)} %centres_ref.1, s32[128]{0:T(128)} %species_ref.1, f32[8,128,128]{2,1,0:T(8,128)S(1)} %bitcast.28, f32[32,8,256]{2,1,0:T(8,128)S(1)} %bitcast.34), custom_call_target="tpu_custom_call" | custom-call | flops 1000000 | bytes 1000000 | tf_op jit(solution)/shard_map/pallas_call | solution.py:385
  42.1 0.1 collective-permute-start
  42.2 1.2 %collective-permute-done = f32[16,128]{1,0:T(8,128)S(1)} collective-permute-done((f32[16,128]{1,0:T(8,128)S(1)}, f32[16,128]{1,0:T(8,128)S(1)}, u32[]{:S(2)}, u32[]{:S(2)}) %collective-permute-start) | collective-permute-done | bytes 8224 | tf_op jit(solution)/shard_map/ppermute | solution.py:30
  43.3 0.3 collective-permute-start.1
  43.7 0.5 shard_map.96.local_ref
  44.1 4.7 %collective-permute-done.1 = f32[16,128]{1,0:T(8,128)S(1)} collective-permute-done((f32[16,128]{1,0:T(8,128)S(1)}, f32[16,128]{1,0:T(8,128)S(1)}, u32[]{:S(2)}, u32[]{:S(2)}) %collective-permute-start.1) | collective-permute-done | bytes 8224 | tf_op jit(solution)/shard_map/ppermute | solution.py:30
  48.8 0.0 collective-permute-start.3
  48.8 3.2 %collective-permute-start.2 = (f32[16,128]{1,0:T(8,128)S(1)}, f32[16,128]{1,0:T(8,128)S(1)}, u32[]{:S(2)}, u32[]{:S(2)}) collective-permute-start(f32[16,128]{1,0:T(8,128)S(1)} %add.51), channel_id=1, source_target_pairs={{0,32},{8,40},{16,48},{24,56},{32,64},{40,72},{48,80},{56,88},{64,... | collective-permute-start | bytes 24584 | tf_op jit(solution)/shard_map/ppermute | solution.py:30
  52.1 3.3 %collective-permute-start.7 = (f32[4,16,128]{2,1,0:T(8,128)S(1)}, f32[4,16,128]{2,1,0:T(8,128)S(1)}, u32[]{:S(2)}, u32[]{:S(2)}) collective-permute-start(f32[4,16,128]{2,1,0:T(8,128)S(1)} %get-tuple-element.14), channel_id=1, source_target_pairs={{0,5},{1,4},{2,7},{3,6},{4,1},{5,0},{6,3},{7,2},{8,13},{9,12},{10,... | collective-permute-start | bytes 98312 | tf_op jit(solution)/shard_map/ppermute | solution.py:30
  55.4 0.8 %collective-permute-start.6 = (f32[4,16,128]{2,1,0:T(8,128)S(1)}, f32[4,16,128]{2,1,0:T(8,128)S(1)}, u32[]{:S(2)}, u32[]{:S(2)}) collective-permute-start(f32[4,16,128]{2,1,0:T(8,128)S(1)} %get-tuple-element.15), channel_id=1, source_target_pairs={{0,1},{1,0},{2,3},{3,2},{4,5},{5,4},{6,7},{7,6},{8,9},{9,8},{10,11... | collective-permute-start | bytes 98312 | tf_op jit(solution)/shard_map/ppermute | solution.py:30
  56.3 1.0 %collective-permute-start.5 = (f32[4,16,128]{2,1,0:T(8,128)S(1)}, f32[4,16,128]{2,1,0:T(8,128)S(1)}, u32[]{:S(2)}, u32[]{:S(2)}) collective-permute-start(f32[4,16,128]{2,1,0:T(8,128)S(1)} %get-tuple-element.16), channel_id=1, source_target_pairs={{0,4},{1,5},{2,6},{3,7},{4,0},{5,1},{6,2},{7,3},{8,12},{9,13},{10,... | collective-permute-start | bytes 98312 | tf_op jit(solution)/shard_map/ppermute | solution.py:30
  57.2 0.7 %copy-done.4 = f32[2,8,8]{2,1,0:T(8,128)S(1)} copy-done((f32[2,8,8]{2,1,0:T(8,128)S(1)}, f32[2,8,8]{2,1,0:T(8,128)}, u32[]{:S(2)}) %copy-start.4) | copy-done | bytes 536
  57.9 4.8 %shard_map.97 = f32[8,128,128]{2,1,0:T(8,128)S(1)} custom-call(s32[816]{0:T(1024)S(1)} %get-tuple-element.7.listed_ref, f32[16,128]{1,0:T(8,128)S(1)} %add_add_fusion.coef_ref, f32[16,8]{1,0:T(8,128)S(1)} %bitcast.35, f32[33,16,128]{2,1,0:T(8,128)S(1)} %get-tuple-element.9.table_ref, f32[8,128,128]{2,1,0:T(8,128)S(1)} %shard_map.96.local_ref), custom_call_target="tpu_custom_call" | custom-call | flops 1000000 | bytes 1000000 | tf_op jit(solution)/shard_map/pallas_call | solution.py:435
  62.7 0.0 collective-permute-done.7.third_ref
  62.7 0.0 collective-permute-done.5.first_ref
  62.8 0.9 %shard_map.101 = (f32[2,4,16,8,128]{4,3,2,1,0:T(8,128)}, f32[4,16,128]{2,1,0:T(8,128)}) custom-call(f32[2,4,16,8,128]{4,3,2,1,0:T(8,128)S(1)} %bitcast.33, f32[2,16,4,8,128]{4,3,2,1,0:T(8,128)S(1)} %bitcast.30, f32[4,16,128]{2,1,0:T(8,128)S(1)} %get-tuple-element.17.mine_ref, f32[4,16,128]{2,1,0:T(8,128)S(1)} %collective-permute-done.5.first_ref, ...), custom_call_target="tpu_custom_call" | custom-call | flops 1000000 | bytes 1000000 | tf_op jit(solution)/shard_map/pallas_call | solution.py:441
  (18 shorter events, 0.1 us)
Async XLA Ops:
  1.9 24.7 %copy-start.1 = (bf16[256,256]{1,0:T(8,128)(2,1)S(1)}, bf16[256,256]{1,0:T(8,128)(2,1)}, u32[]{:S(2)}) copy-start(bf16[256,256]{1,0:T(8,128)(2,1)} %constant.61.clone.wide_ref) | copy-start | bytes 393220
  27.6 9.0 %copy-start = (f32[2,1,4,128,128]{4,3,2,1,0:T(8,128)S(1)}, f32[2,1,4,128,128]{4,3,2,1,0:T(8,128)}, u32[]{:S(2)}) copy-start(f32[2,1,4,128,128]{4,3,2,1,0:T(8,128)} %param.8) | copy-start | bytes 1572868
  27.6 35.1 %all-to-all-start.1 = ((f32[32,4,8,128]{3,2,1,0:T(8,128)}), f32[32,4,8,128]{3,2,1,0:T(8,128)S(1)}, u32[]{:S(2)}, u32[]{:S(2)}) async-start(f32[32,4,8,128]{3,2,1,0:T(8,128)} %bitcast.8), calls=%async_computation.1 | async-start | bytes 1048576 | tf_op jit(solution)/shard_map/all_to_all | solution.py:433
  36.7 1.7 %copy-start.2 = (f32[2,16,8,256]{3,2,1,0:T(8,128)S(1)}, f32[2,16,8,256]{3,2,1,0:T(8,128)}, u32[]{:S(2)}) copy-start(f32[2,16,8,256]{3,2,1,0:T(8,128)} %param.13) | copy-start | bytes 786436
  36.7 15.4 %collective-permute-start.4 = (f32[2,2,4,16,128]{4,3,2,1,0:T(8,128)S(1)}, f32[2,2,4,16,128]{4,3,2,1,0:T(8,128)S(1)}, u32[]{:S(2)}, u32[]{:S(2)}) collective-permute-start(f32[2,2,4,16,128]{4,3,2,1,0:T(8,128)S(1)} %dynamic-slice_bitcast_fusion), channel_id=1, source_target_pairs={{0,2},{1,3},{2,0},{3,1},{4,6},{5,7},{6,4},{7,5},{8,10},{9,11},{10,... | collective-permute-start | bytes 393224 | tf_op jit(solution)/shard_map/ppermute | solution.py:30
  38.4 5.3 %copy-start.3 = (f32[4,128,128]{2,1,0:T(8,128)S(1)}, f32[4,128,128]{2,1,0:T(8,128)}, u32[]{:S(2)}) copy-start(f32[4,128,128]{2,1,0:T(8,128)} %potential_ref.1) | copy-start | bytes 786436
  42.1 1.3 %collective-permute-start = (f32[16,128]{1,0:T(8,128)S(1)}, f32[16,128]{1,0:T(8,128)S(1)}, u32[]{:S(2)}, u32[]{:S(2)}) collective-permute-start(f32[16,128]{1,0:T(8,128)S(1)} %get-tuple-element.8), channel_id=1, source_target_pairs={{0,8},{8,0},{16,24},{24,16},{32,40},{40,32},{48,56},{56,48},{64,72... | collective-permute-start | bytes 24584 | tf_op jit(solution)/shard_map/ppermute | solution.py:30
  43.3 5.5 %collective-permute-start.1 = (f32[16,128]{1,0:T(8,128)S(1)}, f32[16,128]{1,0:T(8,128)S(1)}, u32[]{:S(2)}, u32[]{:S(2)}) collective-permute-start(f32[16,128]{1,0:T(8,128)S(1)} %add.50), channel_id=1, source_target_pairs={{0,16},{8,24},{16,0},{24,8},{32,48},{40,56},{48,32},{56,40},{64,80... | collective-permute-start | bytes 24584 | tf_op jit(solution)/shard_map/ppermute | solution.py:30
  48.8 8.4 %collective-permute-start.3 = (f32[16,128]{1,0:T(8,128)S(1)}, f32[16,128]{1,0:T(8,128)S(1)}, u32[]{:S(2)}, u32[]{:S(2)}) collective-permute-start(f32[16,128]{1,0:T(8,128)S(1)} %add.51), channel_id=1, source_target_pairs={{0,224},{8,232},{16,240},{24,248},{32,0},{40,8},{48,16},{56,24},{6... | collective-permute-start | bytes 24584 | tf_op jit(solution)/shard_map/ppermute | solution.py:30
  48.8 8.4 %collective-permute-start.2 = (f32[16,128]{1,0:T(8,128)S(1)}, f32[16,128]{1,0:T(8,128)S(1)}, u32[]{:S(2)}, u32[]{:S(2)}) collective-permute-start(f32[16,128]{1,0:T(8,128)S(1)} %add.51), channel_id=1, source_target_pairs={{0,32},{8,40},{16,48},{24,56},{32,64},{40,72},{48,80},{56,88},{64,... | collective-permute-start | bytes 24584 | tf_op jit(solution)/shard_map/ppermute | solution.py:30
  52.1 10.6 %collective-permute-start.7 = (f32[4,16,128]{2,1,0:T(8,128)S(1)}, f32[4,16,128]{2,1,0:T(8,128)S(1)}, u32[]{:S(2)}, u32[]{:S(2)}) collective-permute-start(f32[4,16,128]{2,1,0:T(8,128)S(1)} %get-tuple-element.14), channel_id=1, source_target_pairs={{0,5},{1,4},{2,7},{3,6},{4,1},{5,0},{6,3},{7,2},{8,13},{9,12},{10,... | collective-permute-start | bytes 98312 | tf_op jit(solution)/shard_map/ppermute | solution.py:30
  55.4 7.3 %collective-permute-start.6 = (f32[4,16,128]{2,1,0:T(8,128)S(1)}, f32[4,16,128]{2,1,0:T(8,128)S(1)}, u32[]{:S(2)}, u32[]{:S(2)}) collective-permute-start(f32[4,16,128]{2,1,0:T(8,128)S(1)} %get-tuple-element.15), channel_id=1, source_target_pairs={{0,1},{1,0},{2,3},{3,2},{4,5},{5,4},{6,7},{7,6},{8,9},{9,8},{10,11... | collective-permute-start | bytes 98312 | tf_op jit(solution)/shard_map/ppermute | solution.py:30
  56.3 6.5 %collective-permute-start.5 = (f32[4,16,128]{2,1,0:T(8,128)S(1)}, f32[4,16,128]{2,1,0:T(8,128)S(1)}, u32[]{:S(2)}, u32[]{:S(2)}) collective-permute-start(f32[4,16,128]{2,1,0:T(8,128)S(1)} %get-tuple-element.16), channel_id=1, source_target_pairs={{0,4},{1,5},{2,6},{3,7},{4,0},{5,1},{6,2},{7,3},{8,12},{9,13},{10,... | collective-permute-start | bytes 98312 | tf_op jit(solution)/shard_map/ppermute | solution.py:30
  57.2 0.7 %copy-start.4 = (f32[2,8,8]{2,1,0:T(8,128)S(1)}, f32[2,8,8]{2,1,0:T(8,128)}, u32[]{:S(2)}) copy-start(f32[2,8,8]{2,1,0:T(8,128)} %param.14) | copy-start | bytes 1540
